TPU v7x, 32 devices: a whole 2x2x4 slice. The times are simulated.
32 devices in a mesh: dp: 4 (over y, x), section: 2 (over core), ctx: 4 (over z).
Axes of the slice: x: 2, y: 2, z: 4, core: 2. Of those that a mesh axis runs over, the one named last changes fastest.
Arguments:
- queries: bfloat16 [4, 2, 512, 2048], P('dp', 'section', 'ctx'), may hold values from -6 to 6
- key_rows: bfloat16 [4, 2, 512, 128], P('dp', 'section', 'ctx'), may hold values from -6 to 6
- value_rows: bfloat16 [4, 2, 512, 128], P('dp', 'section', 'ctx'), may hold values from -6 to 6
- out_grad: bfloat16 [4, 2, 512, 2048], P('dp', 'section', 'ctx'), may hold values from -6 to 6
- attn_out: bfloat16 [4, 2, 512, 2048], P('dp', 'section', 'ctx'), may hold values from -1.796875 to 1.796875
- log_norm: float32 [4, 2, 512, 16], P('dp', 'section', 'ctx'), may hold values from 2 to 5
- selected: int32 [4, 2, 8, 16], P('dp', 'section', 'ctx'), may hold values from -1 to 7, as said below
- gate_weight: float32 [2, 16, 128], P('section'), may hold values from -0.5 to 0.5
- gate_bias: float32 [2, 16], P('section'), may hold values from -2 to 2
Outputs:
- query_grad_prev: bfloat16 [4, 2, 512, 2048], P('dp', 'section', 'ctx')
- key_grad_prev: bfloat16 [4, 2, 512, 128], P('dp', 'section', 'ctx')
- value_grad_prev: bfloat16 [4, 2, 512, 128], P('dp', 'section', 'ctx')
- gate_weight_grad: float32 [2, 16, 128], P('section')
- gate_bias_grad: float32 [2, 16], P('section')
Inputs may be any that keep to these rules, and one draw needn't show every extreme that they name: `selected`: each row of block b lists distinct blocks of 0 to b, always b itself and block 0, min(16, b + 1) of them, followed by -1 entries.
All inputs are finite; a program needn't handle non-finite values.
Results may differ from a plain program's by a relative error of at most 0.013.
Values may be sent and summed in bfloat16 or wider, within the bound.
No kernel may reach another device: no remote copies, remote signals or barrier semaphores. Data moves between devices by JAX's collectives and lax.ppermute only.
A program may use at most 64 MiB of HBM per device.

v0:
```python
import jax
import jax.numpy as jnp
from jax import lax
from jax.sharding import PartitionSpec as P

BLK = 64
SEL = 16


def from_behind(block, axis, distance):
    devices = range(lax.axis_size(axis))
    route = [(i - distance, i) for i in devices if i - distance in devices]
    return lax.ppermute(block, axis, route)


def block_grads(query_blk, grad_blk, delta_blk, norm_blk, allowed, key_part, value_part, factor):
    scores = jnp.dot(query_blk, key_part.T, preferred_element_type=jnp.float32) * factor
    probs = jnp.where(allowed, jnp.exp(jnp.where(allowed, scores - norm_blk[:, None], 0.0)), 0.0)
    probs_b = probs.astype(jnp.bfloat16)
    dprobs = jnp.dot(grad_blk, value_part.T, preferred_element_type=jnp.float32)
    dscores = (probs * (dprobs - delta_blk[:, None])).astype(jnp.bfloat16)
    query_part = factor * jnp.dot(dscores, key_part, preferred_element_type=jnp.float32)
    key_part_grad = factor * jnp.dot(dscores.T, query_blk, preferred_element_type=jnp.float32)
    value_part_grad = jnp.dot(probs_b.T, grad_blk, preferred_element_type=jnp.float32)
    return (query_part, key_part_grad, value_part_grad)


def on_device(
    queries, key_rows, value_rows, out_grad, attn_out, log_norm, selected, gate_weight, gate_bias
):
    query_mat = queries[0, 0]
    length_dev = query_mat.shape[0]
    head_count = gate_weight.shape[1]
    head_dim = gate_weight.shape[2]
    local_blocks = length_dev // BLK
    chosen = selected[0, 0]
    own_keys = key_rows[0, 0]
    own_values = value_rows[0, 0]
    weight = gate_weight[0]
    factor = head_dim ** (-0.5)
    rank_ctx = lax.axis_index("ctx")
    seq_len = length_dev * lax.axis_size("ctx")
    nblocks = seq_len // BLK
    query3 = query_mat.reshape(length_dev, head_count, head_dim).astype(jnp.float32)
    gate = jax.nn.sigmoid(jnp.sum(query3 * weight[None], axis=-1) + gate_bias[0][None])
    grad3 = out_grad[0, 0].reshape(length_dev, head_count, head_dim).astype(jnp.float32)
    output3 = attn_out[0, 0].reshape(length_dev, head_count, head_dim).astype(jnp.float32)
    branch_grad = (gate[:, :, None] * grad3).astype(jnp.bfloat16)
    row_delta = jnp.sum(branch_grad.astype(jnp.float32) * output3, axis=-1)
    pre_grad = jnp.sum(grad3 * output3, axis=-1) * gate * (1.0 - gate)
    rows_total = length_dev * head_count
    query_flat = query_mat.reshape(rows_total, head_dim)
    grad_flat = branch_grad.reshape(rows_total, head_dim)
    delta_flat = row_delta.reshape(-1)
    norm_flat = log_norm[0, 0].reshape(-1)
    query_pos = rank_ctx * length_dev + jnp.arange(rows_total, dtype=jnp.int32) // head_count
    gate_term = (pre_grad[:, :, None] * weight[None]).reshape(rows_total, head_dim)
    key_all, value_all = (
        lax.all_gather(own_keys, "ctx", axis=0, tiled=True),
        lax.all_gather(own_values, "ctx", axis=0, tiled=True),
    )
    safe_ids = jnp.maximum(chosen, 0)
    key_slots = key_all.reshape(nblocks, BLK, head_dim)[safe_ids].reshape(
        local_blocks, SEL * BLK, head_dim
    )
    value_slots = value_all.reshape(nblocks, BLK, head_dim)[safe_ids].reshape(
        local_blocks, SEL * BLK, head_dim
    )
    block_rows = BLK * head_count

    def one_block(items):
        query_blk, grad_blk, delta_blk, norm_blk, pos_blk, chosen_row, key_part, value_part = items
        key_pos = (
            jnp.maximum(chosen_row, 0)[:, None] * BLK + jnp.arange(BLK, dtype=jnp.int32)[None, :]
        ).reshape(-1)
        usable = jnp.repeat(chosen_row >= 0, BLK)
        allowed = usable[None, :] & (key_pos[None, :] <= pos_blk[:, None])
        return block_grads(
            query_blk, grad_blk, delta_blk, norm_blk, allowed, key_part, value_part, factor
        )

    items = (
        query_flat.reshape(local_blocks, block_rows, head_dim),
        grad_flat.reshape(local_blocks, block_rows, head_dim),
        delta_flat.reshape(local_blocks, block_rows),
        norm_flat.reshape(local_blocks, block_rows),
        query_pos.reshape(local_blocks, block_rows),
        chosen,
        key_slots,
        value_slots,
    )
    query_blocks, key_slot_grad, value_slot_grad = lax.map(one_block, items)
    query_acc = query_blocks.reshape(rows_total, head_dim)
    slot_count = local_blocks * SEL
    both_slots = jnp.concatenate(
        [
            key_slot_grad.reshape(slot_count, BLK, head_dim),
            value_slot_grad.reshape(slot_count, BLK, head_dim),
        ],
        axis=-1,
    ).reshape(slot_count, BLK * 2 * head_dim)
    flat_ids = chosen.reshape(-1)
    block_ids = jnp.arange(seq_len // BLK, dtype=jnp.int32)
    one_hot = (flat_ids[None, :] == block_ids[:, None]).astype(jnp.float32)
    placed = jnp.dot(
        one_hot, both_slots, precision=lax.Precision.HIGHEST, preferred_element_type=jnp.float32
    )
    both_full = placed.reshape(seq_len, 2 * head_dim)
    both_mine = lax.psum_scatter(both_full, "ctx", scatter_dimension=0, tiled=True)
    key_mine = both_mine[:, :head_dim]
    value_mine = both_mine[:, head_dim:]
    query_grad = (
        (query_acc + gate_term).astype(jnp.bfloat16).reshape(length_dev, head_count * head_dim)
    )
    query_sent, key_sent, value_sent = from_behind(
        (query_grad, key_mine.astype(jnp.bfloat16), value_mine.astype(jnp.bfloat16)), "section", -1
    )
    weight_local = jnp.sum(pre_grad[:, :, None] * query3, axis=0)
    bias_local = jnp.sum(pre_grad, axis=0)
    weight_total, bias_total = lax.psum((weight_local, bias_local), ("dp", "ctx"))
    return (
        query_sent[None, None],
        key_sent[None, None],
        value_sent[None, None],
        weight_total[None],
        bias_total[None],
    )


def solution(mesh):
    return jax.shard_map(
        on_device,
        mesh=mesh,
        in_specs=(
            P("dp", "section", "ctx", None),
            P("dp", "section", "ctx", None),
            P("dp", "section", "ctx", None),
            P("dp", "section", "ctx", None),
            P("dp", "section", "ctx", None),
            P("dp", "section", "ctx", None),
            P("dp", "section", "ctx", None),
            P("section", None, None),
            P("section", None),
        ),
        out_specs=(
            P("dp", "section", "ctx", None),
            P("dp", "section", "ctx", None),
            P("dp", "section", "ctx", None),
            P("section", None, None),
            P("section", None),
        ),
        check_vma=False,
    )
```

profile of v0, /device:TPU:0, one launch (start us, length us, event | category | flops | bytes accessed | tf_op | source)
XLA Modules:
  0.0 151.8 jit_solution(7226072562469080117)
XLA Ops:
  7.2 0.8 eq.15
  8.0 0.7 broadcast_maximum_fusion
  8.7 2.2 %convert_bitcast_fusion.2 = f32[16,8,16,128]{3,1,2,0:T(8,128)} fusion(bf16[1,1,128,2048]{3,2,1,0:T(8,128)(2,1)} %param.14), kind=kLoop, calls=%fused_computation.56 | loop fusion | flops 262144 | bytes 1572864
  10.9 1.3 reshape.184
  12.2 1.3 reshape_reshape_squeeze.6
  13.5 0.1 convert_bitcast_fusion
  13.6 0.2 copy.25
  13.8 0.3 multiply_reduce_fusion.2
  14.2 0.1 reduce_sum.50
  14.4 0.1 reshape.189
  14.5 0.1 copy.20
  14.6 0.1 reshape_reshape_squeeze.7
  14.7 0.1 add.89
  14.8 15.1 %all-gather = bf16[1,1,512,128]{3,2,1,0:T(8,128)(2,1)S(1)} all-gather(bf16[1,1,128,128]{3,2,1,0:T(8,128)(2,1)S(1)} %copy-done.10), channel_id=2, replica_groups=mesh['dp'=4,'section'=2,'ctx'=4] {'ctx'}, dimensions={2}, use_global_device_ids=true | all-gather | bytes 163840 | tf_op jit(solution)/shard_map/all_gather | solution.py:59
  29.9 13.5 %all-gather.1 = bf16[1,1,512,128]{3,2,1,0:T(8,128)(2,1)S(1)} all-gather(bf16[1,1,128,128]{3,2,1,0:T(8,128)(2,1)S(1)} %copy-done.11), channel_id=3, replica_groups=mesh['dp'=4,'section'=2,'ctx'=4] {'ctx'}, dimensions={2}, use_global_device_ids=true | all-gather | bytes 163840 | tf_op jit(solution)/shard_map/all_gather | solution.py:60
  43.4 1.4 gather_fusion.1
  44.8 0.6 gather_fusion
  45.5 0.1 convert_bitcast_fusion.1
  45.6 1.2 copy.27
  46.8 1.2 copy.26
  47.9 0.1 add_divide_fusion
  48.0 0.1 copy.22
  48.1 2.5 %multiply_reduce_fusion = (f32[128,16]{1,0:T(8,128)S(1)}, f32[128,16]{1,0:T(8,128)S(1)}) fusion(f32[128,16,128]{2,1,0:T(8,128)} %bitcast.126, f32[128,16,128]{2,1,0:T(8,128)} %bitcast.125, f32[128,16]{1,0:T(8,128)S(1)} %copy.22), kind=kLoop, calls=%fused_computation.51 | loop fusion | flops 1830912 | bytes 2121728 | tf_op jit(solution)/shard_map/reduce_sum | solution.py:50
  50.6 0.1 reshape_reshape.4
  50.7 0.3 multiply_convert_fusion.2
  51.0 18.5 %while.14 = (s32[]{:T(128)}, f32[2,1024,128]{2,1,0:T(8,128)}, f32[2,1024,128]{2,1,0:T(8,128)}, f32[2,1024,128]{2,1,0:T(8,128)}, s32[2,16]{1,0:T(2,128)S(1)}, /*i...) while((s32[]{:T(128)}, f32[2,1024,128]{2,1,0:T(8,128)}, ...), condition=%wide.region_3.4_spmd, body=%wide.region_2.0_spmd.sunk | while | flops 1359217664 | bytes 41232960 | solution.py:92
  51.2 0.1 and.48
  51.4 0.7 fusion.70
  52.2 2.6 %fusion.73 = f32[2,1024,128]{2,1,0:T(8,128)} fusion(f32[2,1024,128]{2,1,0:T(8,128)} %get-tuple-element.199, s32[]{:T(128)S(6)} %copy.38, f32[1024,1024]{1,0:T(8,128)S(1)} %fusion.70, f32[1024]{0:T(1024)S(1)} %bitcast.135, s32[1024]{0:T(1024)S(1)} %add.124, s32[1024]{0:T(1024)S(1)} %bitcast.132, pred[1024]{0:T(1024)(128)(4,1)S(1)} %and.48, ...), kind=kOutput, calls=%fused_computation.7.clone.1 | convolution fusion | flops 275775488 | bytes 4995072 | tf_op jit(solution)/shard_map/while/body/eval_jaxpr/dot_general | solution.py:24
  54.8 2.2 %multiply_convert_fusion.4 = bf16[1024,1024]{1,0:T(8,128)(2,1)S(1)} fusion(f32[1024,1024]{1,0:T(8,128)S(1)} %fusion.70, f32[1024]{0:T(1024)S(1)} %bitcast.134, f32[1024]{0:T(1024)S(1)} %bitcast.136, s32[1024]{0:T(1024)S(1)} %add.124, s32[1024]{0:T(1024)S(1)} %bitcast.133, pred[1024]{0:T(1024)(128)(4,1)S(1)} %and.48, ...), kind=kOutput, calls=%fused_computation.2.clone.1 | convolution fusion | flops 277872640 | bytes 6834176 | tf_op jit(solution)/shard_map/while/body/eval_jaxpr/dot_general | solution.py:20
  57.1 0.8 fusion.72
  57.8 0.4 copy-done.2
  58.3 0.7 fusion.71
  59.0 0.3 copy-done.6
  59.3 1.0 copy-done.3
  60.4 0.1 and.48
  60.6 0.7 fusion.70
  61.4 2.6 %fusion.73 = f32[2,1024,128]{2,1,0:T(8,128)} fusion(f32[2,1024,128]{2,1,0:T(8,128)} %get-tuple-element.199, s32[]{:T(128)S(6)} %copy.38, f32[1024,1024]{1,0:T(8,128)S(1)} %fusion.70, f32[1024]{0:T(1024)S(1)} %bitcast.135, s32[1024]{0:T(1024)S(1)} %add.124, s32[1024]{0:T(1024)S(1)} %bitcast.132, pred[1024]{0:T(1024)(128)(4,1)S(1)} %and.48, ...), kind=kOutput, calls=%fused_computation.7.clone.1 | convolution fusion | flops 275775488 | bytes 4995072 | tf_op jit(solution)/shard_map/while/body/eval_jaxpr/dot_general | solution.py:24
  64.0 2.3 %multiply_convert_fusion.4 = bf16[1024,1024]{1,0:T(8,128)(2,1)S(1)} fusion(f32[1024,1024]{1,0:T(8,128)S(1)} %fusion.70, f32[1024]{0:T(1024)S(1)} %bitcast.134, f32[1024]{0:T(1024)S(1)} %bitcast.136, s32[1024]{0:T(1024)S(1)} %add.124, s32[1024]{0:T(1024)S(1)} %bitcast.133, pred[1024]{0:T(1024)(128)(4,1)S(1)} %and.48, ...), kind=kOutput, calls=%fused_computation.2.clone.1 | convolution fusion | flops 277872640 | bytes 6834176 | tf_op jit(solution)/shard_map/while/body/eval_jaxpr/dot_general | solution.py:20
  66.3 0.8 fusion.72
  67.0 0.4 copy-done.2
  67.5 0.7 fusion.71
  68.2 0.3 copy-done.6
  68.5 1.0 copy-done.3
  69.5 1.7 %pad_maximum_fusion = f32[32,64,256]{2,1,0:T(8,128)S(1)} fusion(f32[32,64,128]{2,1,0:T(8,128)} %bitcast.22, f32[32,64,128]{2,1,0:T(8,128)} %bitcast.130), kind=kLoop, calls=%fused_computation.43 | loop fusion | flops 524288 | bytes 4194304 | tf_op jit(solution)/shard_map/concatenate | solution.py:95
  71.2 1.2 copy.29
  72.4 0.8 fusion.39
  73.3 0.9 reshape.181
  74.2 0.2 fusion.41
  74.4 0.1 copy.24
  74.5 0.2 reshape.177
  74.7 0.3 mul.125
  75.0 0.5 fusion.37
  75.5 1.3 collective-permute-start
  76.8 0.2 mul.130
  77.0 20.3 %reduce-scatter.2.cloned.1.call-done = f32[128,256]{1,0:T(8,128)} async-done(((f32[512,256]{1,0:T(8,128)}), f32[128,256]{1,0:T(8,128)}) %reduce-scatter.2.cloned.1.call-update) | async-done | bytes 131088 | tf_op jit(solution)/shard_map/reduce_scatter | solution.py:109
  97.3 0.9 convert.8
  98.2 1.3 collective-permute-start.2
  99.5 1.3 collective-permute-start.1
  100.8 0.1 fusion.35
  100.9 40.9 %all-reduce = (f32[1,16,128]{2,1,0:T(8,128)}, f32[1,16]{1,0:T(1,128)}) all-reduce(f32[1,16,128]{2,1,0:T(8,128)S(1)} %bitcast.139, f32[1,16]{1,0:T(1,128)S(1)} %bitcast.145), channel_id=1, replica_groups=mesh['dp'=4,'section'=2,'ctx'=4] {'dp','ctx'}, use_global_device_ids=true, to_apply=%region_7.8 | all-reduce | flops 2064 | bytes 16512 | tf_op jit(solution)/shard_map/psum | solution.py:120
  141.8 1.9 %copy.51 = bf16[1,1,128,2048]{3,2,1,0:T(8,128)(2,1)} copy(bf16[1,1,128,2048]{3,2,1,0:T(8,128)(2,1)} %bitcast.20) | data formatting | bytes 1048576
  143.7 0.6 copy.52
  144.3 0.6 copy.53
  (63 shorter events, 0.8 us)
Async XLA Ops:
  7.2 6.3 %copy-start = (bf16[1,1,128,2048]{3,2,1,0:T(8,128)(2,1)S(1)}, bf16[1,1,128,2048]{3,2,1,0:T(8,128)(2,1)}, u32[]{:S(2)}) copy-start(bf16[1,1,128,2048]{3,2,1,0:T(8,128)(2,1)} %param.11) | copy-start | bytes 1572868
  7.2 6.7 %copy-start.9 = (f32[1,16,128]{2,1,0:T(8,128)S(1)}, f32[1,16,128]{2,1,0:T(8,128)}, u32[]{:S(2)}) copy-start(f32[1,16,128]{2,1,0:T(8,128)} %param.18) | copy-start | bytes 24580
  7.2 90.1 %reduce-scatter.2.cloned.1.call-start = ((), (), s32[]{:S(2)}) async-start(), calls=%async_computation.1 | async-start | bytes 655360 | tf_op jit(solution)/shard_map/reduce_scatter | solution.py:109
  8.7 5.8 %copy-start.12 = (f32[1,1,128,16]{2,3,1,0:T(8,128)S(1)}, f32[1,1,128,16]{2,3,1,0:T(8,128)}, u32[]{:S(2)}) copy-start(f32[1,1,128,16]{2,3,1,0:T(8,128)} %param.16) | copy-start | bytes 24580
  10.9 3.8 %copy-start.13 = (f32[1,16]{1,0:T(1,128)S(1)}, f32[1,16]{1,0:T(1,128)}, u32[]{:S(2)}) copy-start(f32[1,16]{1,0:T(1,128)} %param.19) | copy-start | bytes 196
  10.9 4.0 %copy-start.10 = (bf16[1,1,128,128]{3,2,1,0:T(8,128)(2,1)S(1)}, bf16[1,1,128,128]{3,2,1,0:T(8,128)(2,1)}, u32[]{:S(2)}) copy-start(bf16[1,1,128,128]{3,2,1,0:T(8,128)(2,1)} %param.12) | copy-start | bytes 98308
  10.9 19.0 %copy-start.11 = (bf16[1,1,128,128]{3,2,1,0:T(8,128)(2,1)S(1)}, bf16[1,1,128,128]{3,2,1,0:T(8,128)(2,1)}, u32[]{:S(2)}) copy-start(bf16[1,1,128,128]{3,2,1,0:T(8,128)(2,1)} %param.13) | copy-start | bytes 98308
  12.2 33.3 %copy-start.7 = (bf16[1,1,128,2048]{3,2,1,0:T(8,128)(2,1)S(1)}, bf16[1,1,128,2048]{3,2,1,0:T(8,128)(2,1)}, u32[]{:S(2)}) copy-start(bf16[1,1,128,2048]{3,2,1,0:T(8,128)(2,1)} %param.15) | copy-start | bytes 1572868
  45.5 1.3 copy-start.1
  45.6 5.5 %copy-start.14 = (s32[1,1,2,16]{3,2,1,0:T(2,128)S(1)}, s32[1,1,2,16]{3,2,1,0:T(2,128)}, u32[]{:S(2)}) copy-start(s32[1,1,2,16]{3,2,1,0:T(2,128)} %param.17) | copy-start | bytes 388
  52.1 2.6 %copy-start.8 = (bf16[2,1024,128]{2,1,0:T(8,128)(2,1)S(1)}, bf16[2,1024,128]{2,1,0:T(8,128)(2,1)}, u32[]{:S(2)}) copy-start(bf16[2,1024,128]{2,1,0:T(8,128)(2,1)} %get-tuple-element.219) | copy-start | bytes 1572868 | tf_op jit(solution)/shard_map/while
  54.8 2.3 %copy-start.5 = (f32[2,1024,128]{2,1,0:T(8,128)S(1)}, f32[2,1024,128]{2,1,0:T(8,128)}, u32[]{:S(2)}) copy-start(f32[2,1024,128]{2,1,0:T(8,128)} %get-tuple-element.198) | copy-start | bytes 3145732 | tf_op jit(solution)/shard_map/while
  57.0 1.2 copy-start.2
  58.3 1.0 copy-start.6
  59.3 1.0 copy-start.3
  61.4 2.6 %copy-start.8 = (bf16[2,1024,128]{2,1,0:T(8,128)(2,1)S(1)}, bf16[2,1024,128]{2,1,0:T(8,128)(2,1)}, u32[]{:S(2)}) copy-start(bf16[2,1024,128]{2,1,0:T(8,128)(2,1)} %get-tuple-element.219) | copy-start | bytes 1572868 | tf_op jit(solution)/shard_map/while
  64.0 2.3 %copy-start.5 = (f32[2,1024,128]{2,1,0:T(8,128)S(1)}, f32[2,1024,128]{2,1,0:T(8,128)}, u32[]{:S(2)}) copy-start(f32[2,1024,128]{2,1,0:T(8,128)} %get-tuple-element.198) | copy-start | bytes 3145732 | tf_op jit(solution)/shard_map/while
  66.3 1.2 copy-start.2
  67.5 1.0 copy-start.6
  68.5 1.0 copy-start.3
  71.2 3.3 %copy-start.4 = (f32[2,1024,128]{2,1,0:T(8,128)S(1)}, f32[2,1024,128]{2,1,0:T(8,128)}, u32[]{:S(2)}) copy-start(f32[2,1024,128]{2,1,0:T(8,128)} %get-tuple-element.69) | copy-start | bytes 3145732
  75.5 66.3 %collective-permute-start = (bf16[128,2048]{1,0:T(8,128)(2,1)S(1)}, bf16[128,2048]{1,0:T(8,128)(2,1)}, u32[]{:S(2)}, u32[]{:S(2)}) collective-permute-start(bf16[128,2048]{1,0:T(8,128)(2,1)S(1)} %fusion.37), channel_id=1, source_target_pairs={{4,0},{5,1},{6,2},{7,3},{12,8},{13,9},{14,10},{15,11},{20,16},{21,... | collective-permute-start | bytes 1572872 | tf_op jit(solution)/shard_map/ppermute | solution.py:13
  98.2 43.6 %collective-permute-start.2 = (bf16[128,128]{1,0:T(8,128)(2,1)S(1)}, bf16[128,128]{1,0:T(8,128)(2,1)S(1)}, u32[]{:S(2)}, u32[]{:S(2)}) collective-permute-start(bf16[128,128]{1,0:T(8,128)(2,1)S(1)} %get-tuple-element.104), channel_id=1, source_target_pairs={{4,0},{5,1},{6,2},{7,3},{12,8},{13,9},{14,10},{15,11},{20,16},{21,... | collective-permute-start | bytes 98312 | tf_op jit(solution)/shard_map/ppermute | solution.py:13
  99.5 42.3 %collective-permute-start.1 = (bf16[128,128]{1,0:T(8,128)(2,1)S(1)}, bf16[128,128]{1,0:T(8,128)(2,1)S(1)}, u32[]{:S(2)}, u32[]{:S(2)}) collective-permute-start(bf16[128,128]{1,0:T(8,128)(2,1)S(1)} %get-tuple-element.105), channel_id=1, source_target_pairs={{4,0},{5,1},{6,2},{7,3},{12,8},{13,9},{14,10},{15,11},{20,16},{21,... | collective-permute-start | bytes 98312 | tf_op jit(solution)/shard_map/ppermute | solution.py:13
Sparse Core Ops, SparseCore 0:
  74.3 22.9 reduce-scatter.1
where the time goes:
time: 152 us
  blocking collectives  69.4 us (46%)
  waiting for transfers between devices  20.3 us (13%)
  local copies, waits for them, and re-layouts  18.8 us (12%)
  matrix products  14.9 us (10%)
  between operations  14.4 us (9%)
  other arithmetic  9.91 us (7%)
  starting transfers between devices  3.91 us (3%)
    psum x1, blocking collectives, on_device(): lax.psum((weight_local, bias_local), ('dp', 'ctx'))  40.9 us
    reduce_scatter x1, waiting for transfers between devices, on_device(): lax.psum_scatter(both_full, 'ctx', scatter_dimension=0, tiled=True)  20.3 us
    all_gather x1, blocking collectives, on_device(): lax.all_gather(own_keys, 'ctx', axis=0, tiled=True)  15.1 us
    all_gather x1, blocking collectives, on_device(): lax.all_gather(own_values, 'ctx', axis=0, tiled=True)  13.5 us
    unnamed x28, local copies, waits for them, and re-layouts  7 us
    dot_general x2, matrix products, block_grads(): jnp.dot(probs_b.T, grad_blk, preferred_element_type=jnp.float32)  5.24 us
    dot_general x2, matrix products, block_grads(): dprobs = jnp.dot(grad_blk, value_part.T, preferred_element_type=jnp.float32)  4.5 us
    ppermute x3, starting transfers between devices, from_behind(): return lax.ppermute(block, axis, route)  3.88 us
  transfers between devices with their start and end apart: 4, of which 1 were waited for; matrix products, arithmetic and copies ran while one was open for 2% of the time, Pallas kernels for 0%

commit v1 on v0

v1 whole, which is shorter than its diff:
```python
import functools

import jax
import jax.numpy as jnp
from jax import lax
from jax.experimental import pallas as pl
from jax.experimental.pallas import tpu as pltpu
from jax.sharding import PartitionSpec as P

BLK = 64
OUT = 1e30
LOG2E = 1.4426950408889634
NT = (((1,), (1,)), ((), ()))
TN = (((0,), (0,)), ((), ()))
VMEM_BYTES = 48 * 1024 * 1024


def dot32(a, b, dims=(((1,), (0,)), ((), ())), precision=None):
    return lax.dot_general(a, b, dims, precision=precision, preferred_element_type=jnp.float32)


def split16(x):
    high = x.astype(jnp.bfloat16)
    low = (x - high.astype(jnp.float32)).astype(jnp.bfloat16)
    return high, low


def head_blocks(weight):
    heads = weight.shape[0]
    row = lax.broadcasted_iota(jnp.int32, weight.shape, 0)
    return jnp.concatenate([jnp.where(row == h, weight, 0.0) for h in range(heads)], axis=1)


def stats_kernel(query, grad, output, norm, weight, bias, stats, partial):
    heads, head_dim = weight.shape
    length = query.shape[0]
    eye = (
        lax.broadcasted_iota(jnp.int32, (heads, heads), 0)
        == lax.broadcasted_iota(jnp.int32, (heads, heads), 1)
    ).astype(jnp.float32)
    exact = lax.Precision.HIGHEST
    norm_rows = dot32(eye, norm[...], NT, exact)
    bias_col = jnp.sum(eye * bias[...], axis=1, keepdims=True)
    weight_high, weight_low = split16(head_blocks(weight[...]))
    both = dot32(jnp.concatenate([weight_high, weight_low], axis=0), query[...], NT)
    logit = both[:heads] + both[heads:] + bias_col
    product = grad[...].astype(jnp.float32) * output[...].astype(jnp.float32)
    high, low = split16(product)
    ones = head_blocks(jnp.ones((heads, head_dim), jnp.float32)).astype(jnp.bfloat16)
    inner = dot32(ones, high, NT) + dot32(ones, low, NT)
    gate = jax.nn.sigmoid(logit)
    softplus = jnp.maximum(-logit, 0.0) + jnp.log1p(jnp.exp(-jnp.abs(logit)))
    pre_grad = inner * gate * (1.0 - gate)
    stats[0:heads] = LOG2E * (norm_rows + softplus)
    stats[heads : 2 * heads] = inner
    stats[2 * heads : 3 * heads] = pre_grad
    pre_high, pre_low = split16(pre_grad)
    wide = dot32(jnp.concatenate([pre_high, pre_low], axis=0), query[...])
    wide = wide[:heads] + wide[heads:]
    for h in range(heads):
        partial[h : h + 1, :] = wide[h : h + 1, h * head_dim : (h + 1) * head_dim]
    total = jnp.sum(pre_grad, axis=1, keepdims=True)
    lane = lax.broadcasted_iota(jnp.int32, (heads, head_dim), 1)
    row = lax.broadcasted_iota(jnp.int32, (heads, head_dim), 0)
    partial[heads : heads + 8, :] = jnp.broadcast_to(
        jnp.sum(jnp.where(lane == row, total, 0.0), axis=0, keepdims=True), (8, head_dim)
    )


def attention_kernel(count, *refs):
    query, grad, stats, chosen, weight = refs[:5]
    kv = refs[5 : 5 + count]
    query_grad = refs[5 + count]
    kv_grad = refs[6 + count :]
    heads, head_dim = weight.shape
    length = query.shape[0]
    local = length // BLK
    factor = head_dim ** (-0.5)
    rank = lax.axis_index("ctx")
    section = lax.axis_index("section")
    pair = 2 * length
    lane = lax.broadcasted_iota(jnp.int32, (1, length), 1)

    @pl.when(section == 0)
    def _():
        query_grad[...] = jnp.zeros_like(query_grad)
        for ref in kv_grad:
            ref[...] = jnp.zeros_like(ref)

    @pl.when(section > 0)
    def _():
        listed = chosen[...]
        keys = jnp.concatenate([ref[:, :head_dim] for ref in kv], axis=0)
        values = jnp.concatenate([ref[:, head_dim:] for ref in kv], axis=0)
        keys_t = keys.T
        outs = []
        for d in range(count):
            for b in range(local):
                block = lax.rem(rank - d + count, count) * local + b
                hit = jnp.max(jnp.where(listed == block, 1.0, 0.0), axis=1, keepdims=True)
                one = jnp.zeros((1, length), jnp.float32)
                for at in range(local):
                    one = jnp.where(lane // BLK == at, (1.0 - hit[at : at + 1]) * OUT, one)
                outs.append(jnp.broadcast_to(one, (BLK, length)))
        later = lax.broadcasted_iota(jnp.int32, (length, length), 0) > lax.broadcasted_iota(
            jnp.int32, (length, length), 1
        )
        own = jnp.where(later, OUT, jnp.concatenate(outs[:local], axis=0))
        masked = jnp.concatenate([own] + outs[local:], axis=0)
        masked = jnp.concatenate([masked, masked], axis=1)
        weight_high, weight_low = split16(head_blocks(weight[...]))
        pre_high, pre_low = split16(stats[2 * heads : 3 * heads])
        gate_term = dot32(
            jnp.concatenate([pre_high, pre_low, pre_high], axis=0),
            jnp.concatenate([weight_high, weight_high, weight_low], axis=0),
            TN,
        )
        key_acc = jnp.zeros((count * length, head_dim), jnp.float32)
        value_acc = jnp.zeros((count * length, head_dim), jnp.float32)
        for h in range(0, heads, 2):
            first = slice(h * head_dim, (h + 1) * head_dim)
            second = slice((h + 1) * head_dim, (h + 2) * head_dim)
            query_p = jnp.concatenate([query[:, first], query[:, second]], axis=0)
            grad_p = jnp.concatenate([grad[:, first], grad[:, second]], axis=0)
            norm_p = jnp.concatenate([stats[h : h + 1], stats[h + 1 : h + 2]], axis=1)
            inner_p = jnp.concatenate(
                [stats[heads + h : heads + h + 1], stats[heads + h + 1 : heads + h + 2]], axis=1
            )
            scores = dot32(keys, query_p, NT)
            raw = dot32(values, grad_p, NT)
            probs = jnp.exp2(scores * (factor * LOG2E) - (masked + norm_p))
            dscores = (probs * (raw - inner_p)).astype(jnp.bfloat16)
            value_acc += dot32(probs.astype(jnp.bfloat16), grad_p)
            key_acc += dot32(dscores, query_p)
            turned = dot32(keys_t, dscores).T
            query_grad[:, first] = (factor * turned[:length] + gate_term[:, first]).astype(
                jnp.bfloat16
            )
            query_grad[:, second] = (factor * turned[length:] + gate_term[:, second]).astype(
                jnp.bfloat16
            )
        for d, ref in enumerate(kv_grad):
            rows = slice(d * length, (d + 1) * length)
            ref[:, :head_dim] = (factor * key_acc[rows]).astype(jnp.bfloat16)
            ref[:, head_dim:] = value_acc[rows].astype(jnp.bfloat16)


def total_over(array, axis):
    size = lax.axis_size(axis)
    parts = [
        lax.ppermute(array, axis, [(i, (i + d) % size) for i in range(size)])
        for d in range(1, size)
    ]
    return functools.reduce(jnp.add, parts, array)


def on_device(
    queries, key_rows, value_rows, out_grad, attn_out, log_norm, selected, gate_weight, gate_bias
):
    query = queries[0, 0]
    grad = out_grad[0, 0]
    weight = gate_weight[0]
    length, width = query.shape
    heads, head_dim = weight.shape
    size = lax.axis_size("ctx")
    sections = lax.axis_size("section")
    both_axes = ("section", "ctx")
    places = [(s, r) for s in range(sections) for r in range(size)]

    def place(s, r):
        return s * size + r

    own_kv = jnp.concatenate([key_rows[0, 0], value_rows[0, 0]], axis=1)
    kv = [own_kv]
    for d in range(1, size):
        route = [
            (place(s, r), place(s, (r + d) % size) if s else place(s, r)) for s, r in places
        ]
        kv.append(lax.ppermute(own_kv, both_axes, route))
    params = pltpu.CompilerParams(vmem_limit_bytes=VMEM_BYTES)
    stats, partial = pl.pallas_call(
        stats_kernel,
        out_shape=(
            jax.ShapeDtypeStruct((3 * heads, length), jnp.float32),
            jax.ShapeDtypeStruct((heads + 8, head_dim), jnp.float32),
        ),
        compiler_params=params,
        cost_estimate=pl.CostEstimate(
            flops=8 * heads * length * width, transcendentals=0, bytes_accessed=6 * length * width
        ),
        name="gate_stats",
    )(query, grad, attn_out[0, 0], log_norm[0, 0], weight, gate_bias)
    results = pl.pallas_call(
        functools.partial(attention_kernel, size),
        out_shape=(jax.ShapeDtypeStruct((length, width), jnp.bfloat16),)
        + (jax.ShapeDtypeStruct((length, 2 * head_dim), jnp.bfloat16),) * size,
        compiler_params=params,
        cost_estimate=pl.CostEstimate(
            flops=10 * size * length * length * width,
            transcendentals=size * length * length * heads,
            bytes_accessed=6 * length * width,
        ),
        name="attention_grads",
    )(query, grad, stats, selected[0, 0], weight, *kv)
    query_sent = lax.ppermute(
        results[0], "section", [(s, (s - 1) % sections) for s in range(sections)]
    )
    kv_sum = jnp.zeros((length, 2 * head_dim), jnp.float32)
    for d, part in enumerate(results[1:]):
        route = [
            (place(s, r), place(s - 1, (r - d) % size) if s else place(sections - 1, r))
            for s, r in places
        ]
        kv_sum += lax.ppermute(part, both_axes, route).astype(jnp.float32)
    kv_sent = kv_sum.astype(jnp.bfloat16)
    total = total_over(total_over(partial, "dp"), "ctx")
    return (
        query_sent[None, None],
        kv_sent[None, None, :, :head_dim],
        kv_sent[None, None, :, head_dim:],
        total[None, :heads],
        total[heads : heads + 1, :heads],
    )


def solution(mesh):
    rows = P("dp", "section", "ctx", None)
    return jax.shard_map(
        on_device,
        mesh=mesh,
        in_specs=(rows,) * 7 + (P("section", None, None), P("section", None)),
        out_specs=(rows,) * 3 + (P("section", None, None), P("section", None)),
        check_vma=False,
    )
```

time: 152 us -> 42.4 us (0.28)
  blocking collectives: 69.4 us -> 0 us
  starting transfers between devices: 3.91 us -> 23.7 us
  matrix products: 14.9 us -> 0 us
  between operations: 14.4 us -> 0.76 us
  waiting for transfers between devices: 20.3 us -> 8.75 us
  local copies, waits for them, and re-layouts: 18.8 us -> 7.83 us
  other arithmetic: 9.91 us -> 0.06 us
    psum x1 -> x0, blocking collectives: 40.9 us -> none  [on_device(): lax.psum((weight_local, bias_local), ('dp', 'ctx'))]
    all_gather x2 -> x0, blocking collectives: 28.5 us -> none  [the longest x1 15.1 us: on_device(): lax.all_gather(own_keys, 'ctx', axis=0, tiled=True)]
    reduce_scatter x1 -> x0, waiting for transfers between devices: 20.3 us -> none  [on_device(): lax.psum_scatter(both_full, 'ctx', scatter_dimension=0, tiled=True)]
    ppermute x3 -> x14, starting transfers between devices: 3.88 us -> 23.7 us  [the longest x4 10.2 us: on_device(): kv_sum += lax.ppermute(part, both_axes, route).astype(jnp.float32)]
    dot_general x11 -> x0, matrix products: 14.9 us -> none  [the longest x2 5.24 us: block_grads(): jnp.dot(probs_b.T, grad_blk, preferred_element_type=jnp.float32)]
    ppermute x3 -> x14, waiting for transfers between devices: 0.01 us -> 8.75 us  [the longest x6 6.49 us: total_over(): lax.ppermute(array, axis, [(i, (i + d) % size) for i in range(size)])]
    while x20 -> x0, local copies, waits for them, and re-layouts: 3.49 us -> none
    reduce_sum x4 -> x0, other arithmetic: 3.13 us -> none  [the longest x1 2.45 us: on_device(): pre_grad = jnp.sum(grad3 * output3, axis=-1) * gate * (1.0 - gate)]
  transfers between devices with their start and end apart: 4 -> 14, of which waited for: 1 -> 8; matrix products, arithmetic and copies ran while one was open for 2% -> 4% of each run, Pallas kernels for 0% -> 0%
where the time goes in v1:
time: 42.4 us; the launch traced here: 42 us
  starting transfers between devices  23.7 us (56%)
  waiting for transfers between devices  8.75 us (21%)
  local copies, waits for them, and re-layouts  7.83 us (18%)
  Pallas kernels  0.96 us (2%)
  between operations  0.76 us (2%)
    ppermute x4, starting transfers between devices, on_device(): kv_sum += lax.ppermute(part, both_axes, route).astype(jnp.float32)  10.2 us
    ppermute x6, starting transfers between devices, total_over(): lax.ppermute(array, axis, [(i, (i + d) % size) for i in range(size)])  9.66 us
    ppermute x6, waiting for transfers between devices, total_over(): lax.ppermute(array, axis, [(i, (i + d) % size) for i in range(size)])  6.49 us
    unnamed x18, local copies, waits for them, and re-layouts  6.09 us
    ppermute x4, waiting for transfers between devices, on_device(): kv_sum += lax.ppermute(part, both_axes, route).astype(jnp.float32)  2.25 us
    ppermute x3, starting transfers between devices, on_device(): kv.append(lax.ppermute(own_kv, both_axes, route))  1.99 us
    ppermute x1, starting transfers between devices, on_device(): lax.ppermute(results[0], 'section', [(s, (s - 1) % sections) for s in ran...  1.79 us
    pallas_call x1, Pallas kernels, on_device(): pl.pallas_call(stats_kernel, out_shape=(jax.ShapeDtypeStruct((3 * heads,...  0.9 us
  transfers between devices with their start and end apart: 14, of which 8 were waited for; matrix products, arithmetic and copies ran while one was open for 4% of the time, Pallas kernels for 0%

profile of v1, /device:TPU:0, one launch (start us, length us, event | category | flops | bytes accessed | tf_op | source)
XLA Modules:
  0.0 42.0 jit_solution(1227816322805984566)
XLA Ops:
  0.6 0.8 %copy.14 = f32[1,1,128,16]{3,2,1,0:T(8,128)S(1)} copy(f32[1,1,128,16]{2,3,1,0:T(8,128)} %param.14) | data formatting | bytes 16384 | tf_op args[5]
  1.4 0.0 copy-start.3
  1.4 0.0 copy-start.4
  1.4 0.7 %copy-done.3 = f32[1,16,128]{2,1,0:T(8,128)S(1)} copy-done((f32[1,16,128]{2,1,0:T(8,128)S(1)}, f32[1,16,128]{2,1,0:T(8,128)}, u32[]{:S(2)}) %copy-start.3) | copy-done | bytes 8216
  2.1 0.0 copy-done.4
  2.1 0.0 copy-start
  2.1 1.0 %copy-done = bf16[1,1,128,2048]{3,2,1,0:T(8,128)(2,1)S(1)} copy-done((bf16[1,1,128,2048]{3,2,1,0:T(8,128)(2,1)S(1)}, bf16[1,1,128,2048]{3,2,1,0:T(8,128)(2,1)}, u32[]{:S(2)}) %copy-start) | copy-done | bytes 524312
  3.2 0.0 copy-start.1
  3.2 1.0 %copy-done.1 = bf16[1,1,128,2048]{3,2,1,0:T(8,128)(2,1)S(1)} copy-done((bf16[1,1,128,2048]{3,2,1,0:T(8,128)(2,1)S(1)}, bf16[1,1,128,2048]{3,2,1,0:T(8,128)(2,1)}, u32[]{:S(2)}) %copy-start.1) | copy-done | bytes 524312
  4.2 0.0 copy-start.2
  4.2 1.0 %copy-done.2 = bf16[1,1,128,2048]{3,2,1,0:T(8,128)(2,1)S(1)} copy-done((bf16[1,1,128,2048]{3,2,1,0:T(8,128)(2,1)S(1)}, bf16[1,1,128,2048]{3,2,1,0:T(8,128)(2,1)}, u32[]{:S(2)}) %copy-start.2) | copy-done | bytes 524312
  5.3 0.9 %gate_stats.1 = (f32[48,128]{1,0:T(8,128)S(1)}, f32[24,128]{1,0:T(8,128)S(1)}) custom-call(bf16[128,2048]{1,0:T(8,128)(2,1)S(1)} %bitcast.16, bf16[128,2048]{1,0:T(8,128)(2,1)S(1)} %bitcast.18, bf16[128,2048]{1,0:T(8,128)(2,1)S(1)} %bitcast.15, f32[128,16]{1,0:T(8,128)S(1)} %bitcast.20, f32[16,128]{1,0:T(8,128)S(1)} %bitcast.21, f32[1,16]{1,0:T(1,128)S(1)} %copy-done.4), custom_call_target="tpu_custom_call" | custom-call | flops 33554432 | bytes 1572864 | tf_op jit(solution)/shard_map/gate_stats/pallas_call | solution.py:181
  6.2 0.0 copy-start.7
  6.2 0.0 copy-start.6
  6.2 3.9 %collective-permute-start.10 = (f32[24,128]{1,0:T(8,128)S(1)}, f32[24,128]{1,0:T(8,128)S(1)}, u32[]{:S(2)}, u32[]{:S(2)}) collective-permute-start(f32[24,128]{1,0:T(8,128)S(1)} %get-tuple-element.18), channel_id=1, source_target_pairs={{0,24},{8,0},{16,8},{24,16},{1,25},{9,1},{17,9},{25,17},{2,26},{10... | collective-permute-start | bytes 36872 | tf_op jit(solution)/shard_map/ppermute | solution.py:151
  10.1 0.5 %collective-permute-start.9 = (f32[24,128]{1,0:T(8,128)S(1)}, f32[24,128]{1,0:T(8,128)S(1)}, u32[]{:S(2)}, u32[]{:S(2)}) collective-permute-start(f32[24,128]{1,0:T(8,128)S(1)} %get-tuple-element.18), channel_id=1, source_target_pairs={{0,16},{8,24},{16,0},{24,8},{1,17},{9,25},{17,1},{25,9},{2,18},{10... | collective-permute-start | bytes 36872 | tf_op jit(solution)/shard_map/ppermute | solution.py:151
  10.7 0.6 %collective-permute-start.8 = (f32[24,128]{1,0:T(8,128)S(1)}, f32[24,128]{1,0:T(8,128)S(1)}, u32[]{:S(2)}, u32[]{:S(2)}) collective-permute-start(f32[24,128]{1,0:T(8,128)S(1)} %get-tuple-element.18), channel_id=1, source_target_pairs={{0,8},{8,16},{16,24},{24,0},{1,9},{9,17},{17,25},{25,1},{2,10},{10... | collective-permute-start | bytes 36872 | tf_op jit(solution)/shard_map/ppermute | solution.py:151
  11.2 0.3 collective-permute-done.10
  11.5 2.3 %collective-permute-done.9 = f32[24,128]{1,0:T(8,128)S(1)} collective-permute-done((f32[24,128]{1,0:T(8,128)S(1)}, f32[24,128]{1,0:T(8,128)S(1)}, u32[]{:S(2)}, u32[]{:S(2)}) %collective-permute-start.9) | collective-permute-done | bytes 12320 | tf_op jit(solution)/shard_map/ppermute | solution.py:151
  13.8 1.4 %collective-permute-done.8 = f32[24,128]{1,0:T(8,128)S(1)} collective-permute-done((f32[24,128]{1,0:T(8,128)S(1)}, f32[24,128]{1,0:T(8,128)S(1)}, u32[]{:S(2)}, u32[]{:S(2)}) %collective-permute-start.8) | collective-permute-done | bytes 12320 | tf_op jit(solution)/shard_map/ppermute | solution.py:151
  15.3 3.6 %collective-permute-start.13 = (f32[24,128]{1,0:T(8,128)S(1)}, f32[24,128]{1,0:T(8,128)S(1)}, u32[]{:S(2)}, u32[]{:S(2)}) collective-permute-start(f32[24,128]{1,0:T(8,128)S(1)} %add_add_fusion.1), channel_id=1, source_target_pairs={{0,3},{1,0},{2,1},{3,2},{4,7},{5,4},{6,5},{7,6},{8,11},{9,8},{10,9... | collective-permute-start | bytes 36872 | tf_op jit(solution)/shard_map/ppermute | solution.py:151
  18.9 0.0 collective-permute-start.12
  18.9 1.0 %collective-permute-start.11 = (f32[24,128]{1,0:T(8,128)S(1)}, f32[24,128]{1,0:T(8,128)S(1)}, u32[]{:S(2)}, u32[]{:S(2)}) collective-permute-start(f32[24,128]{1,0:T(8,128)S(1)} %add_add_fusion.1), channel_id=1, source_target_pairs={{0,1},{1,2},{2,3},{3,0},{4,5},{5,6},{6,7},{7,4},{8,9},{9,10},{10,1... | collective-permute-start | bytes 36872 | tf_op jit(solution)/shard_map/ppermute | solution.py:151
  19.9 0.0 copy-done.7
  19.9 0.0 copy-done.6
  19.9 0.7 %collective-permute-start.2 = (bf16[128,256]{1,0:T(8,128)(2,1)S(1)}, bf16[128,256]{1,0:T(8,128)(2,1)S(1)}, u32[]{:S(2)}, u32[]{:S(2)}) collective-permute-start(bf16[128,256]{1,0:T(8,128)(2,1)S(1)} %pad_maximum_fusion.refs_5_), channel_id=1, source_target_pairs={{0,0},{1,1},{2,2},{3,3},{4,7},{5,4},{6,5},{7,6},{8,8},{9,9},{10,10... | collective-permute-start | bytes 196616 | tf_op jit(solution)/shard_map/ppermute | solution.py:179
  20.6 0.7 %collective-permute-start.1 = (bf16[128,256]{1,0:T(8,128)(2,1)S(1)}, bf16[128,256]{1,0:T(8,128)(2,1)S(1)}, u32[]{:S(2)}, u32[]{:S(2)}) collective-permute-start(bf16[128,256]{1,0:T(8,128)(2,1)S(1)} %pad_maximum_fusion.refs_5_), channel_id=1, source_target_pairs={{0,0},{1,1},{2,2},{3,3},{4,6},{5,7},{6,4},{7,5},{8,8},{9,9},{10,10... | collective-permute-start | bytes 196616 | tf_op jit(solution)/shard_map/ppermute | solution.py:179
  21.2 0.0 collective-permute-done.13
  21.2 0.7 %collective-permute-start = (bf16[128,256]{1,0:T(8,128)(2,1)S(1)}, bf16[128,256]{1,0:T(8,128)(2,1)S(1)}, u32[]{:S(2)}, u32[]{:S(2)}) collective-permute-start(bf16[128,256]{1,0:T(8,128)(2,1)S(1)} %pad_maximum_fusion.refs_5_), channel_id=1, source_target_pairs={{0,0},{1,1},{2,2},{3,3},{4,5},{5,6},{6,7},{7,4},{8,8},{9,9},{10,10... | collective-permute-start | bytes 196616 | tf_op jit(solution)/shard_map/ppermute | solution.py:179
  21.9 1.5 %collective-permute-done.12 = f32[24,128]{1,0:T(8,128)S(1)} collective-permute-done((f32[24,128]{1,0:T(8,128)S(1)}, f32[24,128]{1,0:T(8,128)S(1)}, u32[]{:S(2)}, u32[]{:S(2)}) %collective-permute-start.12) | collective-permute-done | bytes 12320 | tf_op jit(solution)/shard_map/ppermute | solution.py:151
  23.4 1.0 %collective-permute-done.11 = f32[24,128]{1,0:T(8,128)S(1)} collective-permute-done((f32[24,128]{1,0:T(8,128)S(1)}, f32[24,128]{1,0:T(8,128)S(1)}, u32[]{:S(2)}, u32[]{:S(2)}) %collective-permute-start.11) | collective-permute-done | bytes 12320 | tf_op jit(solution)/shard_map/ppermute | solution.py:151
  24.4 0.0 collective-permute-done.2.refs_8_
  24.4 0.0 collective-permute-done.1.refs_7_
  24.4 0.0 collective-permute-done.refs_6_
  24.4 0.0 copy-start.5
  24.4 0.7 %copy-done.5 = s32[1,1,2,16]{3,2,1,0:T(2,128)S(1)} copy-done((s32[1,1,2,16]{3,2,1,0:T(2,128)S(1)}, s32[1,1,2,16]{3,2,1,0:T(2,128)}, u32[]{:S(2)}) %copy-start.5) | copy-done | bytes 152
  25.1 0.1 attention_grads.1
  25.2 9.8 %collective-permute-start.4 = (bf16[128,256]{1,0:T(8,128)(2,1)S(1)}, bf16[128,256]{1,0:T(8,128)(2,1)S(1)}, u32[]{:S(2)}, u32[]{:S(2)}) collective-permute-start(bf16[128,256]{1,0:T(8,128)(2,1)S(1)} %get-tuple-element.14), channel_id=1, source_target_pairs={{0,4},{1,5},{2,6},{3,7},{4,0},{5,1},{6,2},{7,3},{8,12},{9,13},{10,... | collective-permute-start | bytes 196616 | tf_op jit(solution)/shard_map/ppermute | solution.py:214
  35.0 0.1 collective-permute-start.5
  35.0 0.1 collective-permute-start.6
  35.1 0.3 collective-permute-start.7
  35.4 1.8 %collective-permute-start.3 = (bf16[128,2048]{1,0:T(8,128)(2,1)S(1)}, bf16[128,2048]{1,0:T(8,128)(2,1)S(1)}, u32[]{:S(2)}, u32[]{:S(2)}) collective-permute-start(bf16[128,2048]{1,0:T(8,128)(2,1)S(1)} %get-tuple-element.13), channel_id=1, source_target_pairs={{0,4},{4,0},{1,5},{5,1},{2,6},{6,2},{3,7},{7,3},{8,12},{12,8},{9,1... | collective-permute-start | bytes 1572872 | tf_op jit(solution)/shard_map/ppermute | solution.py:205
  37.2 0.6 %slice_bitcast_fusion.2 = f32[1,16,128]{2,1,0:T(8,128)} fusion(f32[24,128]{1,0:T(8,128)S(1)} %add_add_fusion), kind=kLoop, calls=%fused_computation.6 | loop fusion | bytes 16384 | tf_op jit(solution)/shard_map/broadcast_in_dim | solution.py:221
  37.8 0.5 %slice.19 = f32[1,16]{1,0:T(1,128)} slice(f32[24,128]{1,0:T(8,128)S(1)} %add_add_fusion), slice={[16:17], [0:16]} | slice | bytes 128 | tf_op jit(solution)/shard_map/slice | solution.py:222
  38.3 0.0 collective-permute-done.4
  38.3 0.3 collective-permute-done.5
  38.6 1.1 %collective-permute-done.6 = bf16[128,256]{1,0:T(8,128)(2,1)S(1)} collective-permute-done((bf16[128,256]{1,0:T(8,128)(2,1)S(1)}, bf16[128,256]{1,0:T(8,128)(2,1)S(1)}, u32[]{:S(2)}, u32[]{:S(2)}) %collective-permute-start.6) | collective-permute-done | bytes 65568 | tf_op jit(solution)/shard_map/ppermute | solution.py:214
  39.8 0.8 %collective-permute-done.7 = bf16[128,256]{1,0:T(8,128)(2,1)S(1)} collective-permute-done((bf16[128,256]{1,0:T(8,128)(2,1)S(1)}, bf16[128,256]{1,0:T(8,128)(2,1)S(1)}, u32[]{:S(2)}, u32[]{:S(2)}) %collective-permute-start.7) | collective-permute-done | bytes 65568 | tf_op jit(solution)/shard_map/ppermute | solution.py:214
  40.6 0.6 %slice_bitcast_fusion = (bf16[1,1,128,128]{3,2,1,0:T(8,128)(2,1)}, bf16[1,1,128,128]{3,2,1,0:T(8,128)(2,1)}) fusion(bf16[128,256]{1,0:T(8,128)(2,1)S(1)} %add_convert_fusion), kind=kLoop, calls=%fused_computation.2 | loop fusion | bytes 131072 | tf_op jit(solution)/shard_map/broadcast_in_dim | solution.py:220
  41.2 0.0 collective-permute-done.3
  41.3 0.8 %copy.16 = bf16[1,1,128,2048]{3,2,1,0:T(8,128)(2,1)} copy(bf16[1,1,128,2048]{3,2,1,0:T(8,128)(2,1)S(1)} %bitcast.24) | data formatting | bytes 1048576
  (4 shorter events, 0.1 us)
Async XLA Ops:
  1.4 0.7 %copy-start.3 = (f32[1,16,128]{2,1,0:T(8,128)S(1)}, f32[1,16,128]{2,1,0:T(8,128)}, u32[]{:S(2)}) copy-start(f32[1,16,128]{2,1,0:T(8,128)} %param.16) | copy-start | bytes 24580
  1.4 0.7 %copy-start.4 = (f32[1,16]{1,0:T(1,128)S(1)}, f32[1,16]{1,0:T(1,128)}, u32[]{:S(2)}) copy-start(f32[1,16]{1,0:T(1,128)} %bias.1) | copy-start | bytes 196
  2.1 1.0 %copy-start = (bf16[1,1,128,2048]{3,2,1,0:T(8,128)(2,1)S(1)}, bf16[1,1,128,2048]{3,2,1,0:T(8,128)(2,1)}, u32[]{:S(2)}) copy-start(bf16[1,1,128,2048]{3,2,1,0:T(8,128)(2,1)} %param.13) | copy-start | bytes 1572868
  3.2 1.0 %copy-start.1 = (bf16[1,1,128,2048]{3,2,1,0:T(8,128)(2,1)S(1)}, bf16[1,1,128,2048]{3,2,1,0:T(8,128)(2,1)}, u32[]{:S(2)}) copy-start(bf16[1,1,128,2048]{3,2,1,0:T(8,128)(2,1)} %param.9) | copy-start | bytes 1572868
  4.2 1.0 %copy-start.2 = (bf16[1,1,128,2048]{3,2,1,0:T(8,128)(2,1)S(1)}, bf16[1,1,128,2048]{3,2,1,0:T(8,128)(2,1)}, u32[]{:S(2)}) copy-start(bf16[1,1,128,2048]{3,2,1,0:T(8,128)(2,1)} %param.12) | copy-start | bytes 1572868
  6.2 13.7 %copy-start.7 = (bf16[1,1,128,128]{3,2,1,0:T(8,128)(2,1)S(1)}, bf16[1,1,128,128]{3,2,1,0:T(8,128)(2,1)}, u32[]{:S(2)}) copy-start(bf16[1,1,128,128]{3,2,1,0:T(8,128)(2,1)} %param.10) | copy-start | bytes 98308
  6.2 13.7 %copy-start.6 = (bf16[1,1,128,128]{3,2,1,0:T(8,128)(2,1)S(1)}, bf16[1,1,128,128]{3,2,1,0:T(8,128)(2,1)}, u32[]{:S(2)}) copy-start(bf16[1,1,128,128]{3,2,1,0:T(8,128)(2,1)} %param.11) | copy-start | bytes 98308
  6.2 5.4 %collective-permute-start.10 = (f32[24,128]{1,0:T(8,128)S(1)}, f32[24,128]{1,0:T(8,128)S(1)}, u32[]{:S(2)}, u32[]{:S(2)}) collective-permute-start(f32[24,128]{1,0:T(8,128)S(1)} %get-tuple-element.18), channel_id=1, source_target_pairs={{0,24},{8,0},{16,8},{24,16},{1,25},{9,1},{17,9},{25,17},{2,26},{10... | collective-permute-start | bytes 36872 | tf_op jit(solution)/shard_map/ppermute | solution.py:151
  10.1 3.7 %collective-permute-start.9 = (f32[24,128]{1,0:T(8,128)S(1)}, f32[24,128]{1,0:T(8,128)S(1)}, u32[]{:S(2)}, u32[]{:S(2)}) collective-permute-start(f32[24,128]{1,0:T(8,128)S(1)} %get-tuple-element.18), channel_id=1, source_target_pairs={{0,16},{8,24},{16,0},{24,8},{1,17},{9,25},{17,1},{25,9},{2,18},{10... | collective-permute-start | bytes 36872 | tf_op jit(solution)/shard_map/ppermute | solution.py:151
  10.7 4.6 %collective-permute-start.8 = (f32[24,128]{1,0:T(8,128)S(1)}, f32[24,128]{1,0:T(8,128)S(1)}, u32[]{:S(2)}, u32[]{:S(2)}) collective-permute-start(f32[24,128]{1,0:T(8,128)S(1)} %get-tuple-element.18), channel_id=1, source_target_pairs={{0,8},{8,16},{16,24},{24,0},{1,9},{9,17},{17,25},{25,1},{2,10},{10... | collective-permute-start | bytes 36872 | tf_op jit(solution)/shard_map/ppermute | solution.py:151
  15.3 6.0 %collective-permute-start.13 = (f32[24,128]{1,0:T(8,128)S(1)}, f32[24,128]{1,0:T(8,128)S(1)}, u32[]{:S(2)}, u32[]{:S(2)}) collective-permute-start(f32[24,128]{1,0:T(8,128)S(1)} %add_add_fusion.1), channel_id=1, source_target_pairs={{0,3},{1,0},{2,1},{3,2},{4,7},{5,4},{6,5},{7,6},{8,11},{9,8},{10,9... | collective-permute-start | bytes 36872 | tf_op jit(solution)/shard_map/ppermute | solution.py:151
  18.9 4.6 %collective-permute-start.12 = (f32[24,128]{1,0:T(8,128)S(1)}, f32[24,128]{1,0:T(8,128)S(1)}, u32[]{:S(2)}, u32[]{:S(2)}) collective-permute-start(f32[24,128]{1,0:T(8,128)S(1)} %add_add_fusion.1), channel_id=1, source_target_pairs={{0,2},{1,3},{2,0},{3,1},{4,6},{5,7},{6,4},{7,5},{8,10},{9,11},{10,... | collective-permute-start | bytes 36872 | tf_op jit(solution)/shard_map/ppermute | solution.py:151
  18.9 5.5 %collective-permute-start.11 = (f32[24,128]{1,0:T(8,128)S(1)}, f32[24,128]{1,0:T(8,128)S(1)}, u32[]{:S(2)}, u32[]{:S(2)}) collective-permute-start(f32[24,128]{1,0:T(8,128)S(1)} %add_add_fusion.1), channel_id=1, source_target_pairs={{0,1},{1,2},{2,3},{3,0},{4,5},{5,6},{6,7},{7,4},{8,9},{9,10},{10,1... | collective-permute-start | bytes 36872 | tf_op jit(solution)/shard_map/ppermute | solution.py:151
  19.9 4.5 %collective-permute-start.2 = (bf16[128,256]{1,0:T(8,128)(2,1)S(1)}, bf16[128,256]{1,0:T(8,128)(2,1)S(1)}, u32[]{:S(2)}, u32[]{:S(2)}) collective-permute-start(bf16[128,256]{1,0:T(8,128)(2,1)S(1)} %pad_maximum_fusion.refs_5_), channel_id=1, source_target_pairs={{0,0},{1,1},{2,2},{3,3},{4,7},{5,4},{6,5},{7,6},{8,8},{9,9},{10,10... | collective-permute-start | bytes 196616 | tf_op jit(solution)/shard_map/ppermute | solution.py:179
  20.6 3.9 %collective-permute-start.1 = (bf16[128,256]{1,0:T(8,128)(2,1)S(1)}, bf16[128,256]{1,0:T(8,128)(2,1)S(1)}, u32[]{:S(2)}, u32[]{:S(2)}) collective-permute-start(bf16[128,256]{1,0:T(8,128)(2,1)S(1)} %pad_maximum_fusion.refs_5_), channel_id=1, source_target_pairs={{0,0},{1,1},{2,2},{3,3},{4,6},{5,7},{6,4},{7,5},{8,8},{9,9},{10,10... | collective-permute-start | bytes 196616 | tf_op jit(solution)/shard_map/ppermute | solution.py:179
  21.2 3.2 %collective-permute-start = (bf16[128,256]{1,0:T(8,128)(2,1)S(1)}, bf16[128,256]{1,0:T(8,128)(2,1)S(1)}, u32[]{:S(2)}, u32[]{:S(2)}) collective-permute-start(bf16[128,256]{1,0:T(8,128)(2,1)S(1)} %pad_maximum_fusion.refs_5_), channel_id=1, source_target_pairs={{0,0},{1,1},{2,2},{3,3},{4,5},{5,6},{6,7},{7,4},{8,8},{9,9},{10,10... | collective-permute-start | bytes 196616 | tf_op jit(solution)/shard_map/ppermute | solution.py:179
  24.4 0.7 %copy-start.5 = (s32[1,1,2,16]{3,2,1,0:T(2,128)S(1)}, s32[1,1,2,16]{3,2,1,0:T(2,128)}, u32[]{:S(2)}) copy-start(s32[1,1,2,16]{3,2,1,0:T(2,128)} %param.15) | copy-start | bytes 388
  25.2 13.1 %collective-permute-start.4 = (bf16[128,256]{1,0:T(8,128)(2,1)S(1)}, bf16[128,256]{1,0:T(8,128)(2,1)S(1)}, u32[]{:S(2)}, u32[]{:S(2)}) collective-permute-start(bf16[128,256]{1,0:T(8,128)(2,1)S(1)} %get-tuple-element.14), channel_id=1, source_target_pairs={{0,4},{1,5},{2,6},{3,7},{4,0},{5,1},{6,2},{7,3},{8,12},{9,13},{10,... | collective-permute-start | bytes 196616 | tf_op jit(solution)/shard_map/ppermute | solution.py:214
  35.0 3.7 %collective-permute-start.5 = (bf16[128,256]{1,0:T(8,128)(2,1)S(1)}, bf16[128,256]{1,0:T(8,128)(2,1)S(1)}, u32[]{:S(2)}, u32[]{:S(2)}) collective-permute-start(bf16[128,256]{1,0:T(8,128)(2,1)S(1)} %get-tuple-element.15), channel_id=1, source_target_pairs={{0,4},{1,5},{2,6},{3,7},{4,3},{5,0},{6,1},{7,2},{8,12},{9,13},{10,... | collective-permute-start | bytes 196616 | tf_op jit(solution)/shard_map/ppermute | solution.py:214
  35.0 4.7 %collective-permute-start.6 = (bf16[128,256]{1,0:T(8,128)(2,1)S(1)}, bf16[128,256]{1,0:T(8,128)(2,1)S(1)}, u32[]{:S(2)}, u32[]{:S(2)}) collective-permute-start(bf16[128,256]{1,0:T(8,128)(2,1)S(1)} %get-tuple-element.16), channel_id=1, source_target_pairs={{0,4},{1,5},{2,6},{3,7},{4,2},{5,3},{6,0},{7,1},{8,12},{9,13},{10,... | collective-permute-start | bytes 196616 | tf_op jit(solution)/shard_map/ppermute | solution.py:214
  35.1 5.5 %collective-permute-start.7 = (bf16[128,256]{1,0:T(8,128)(2,1)S(1)}, bf16[128,256]{1,0:T(8,128)(2,1)S(1)}, u32[]{:S(2)}, u32[]{:S(2)}) collective-permute-start(bf16[128,256]{1,0:T(8,128)(2,1)S(1)} %get-tuple-element.17), channel_id=1, source_target_pairs={{0,4},{1,5},{2,6},{3,7},{4,1},{5,2},{6,3},{7,0},{8,12},{9,13},{10,... | collective-permute-start | bytes 196616 | tf_op jit(solution)/shard_map/ppermute | solution.py:214
  35.4 5.8 %collective-permute-start.3 = (bf16[128,2048]{1,0:T(8,128)(2,1)S(1)}, bf16[128,2048]{1,0:T(8,128)(2,1)S(1)}, u32[]{:S(2)}, u32[]{:S(2)}) collective-permute-start(bf16[128,2048]{1,0:T(8,128)(2,1)S(1)} %get-tuple-element.13), channel_id=1, source_target_pairs={{0,4},{4,0},{1,5},{5,1},{2,6},{6,2},{3,7},{7,3},{8,12},{12,8},{9,1... | collective-permute-start | bytes 1572872 | tf_op jit(solution)/shard_map/ppermute | solution.py:205

commit v2 on v1

v2 whole, which is shorter than its diff:
```python
import functools

import jax
import jax.numpy as jnp
from jax import lax
from jax.experimental import pallas as pl
from jax.experimental.pallas import tpu as pltpu
from jax.sharding import PartitionSpec as P

BLK = 64
OUT = 1e30
LOG2E = 1.4426950408889634
NT = (((1,), (1,)), ((), ()))
TN = (((0,), (0,)), ((), ()))
VMEM_BYTES = 48 * 1024 * 1024


def dot32(a, b, dims=(((1,), (0,)), ((), ())), precision=None):
    return lax.dot_general(a, b, dims, precision=precision, preferred_element_type=jnp.float32)


def split16(x):
    high = x.astype(jnp.bfloat16)
    low = (x - high.astype(jnp.float32)).astype(jnp.bfloat16)
    return high, low


def head_blocks(weight):
    heads = weight.shape[0]
    row = lax.broadcasted_iota(jnp.int32, weight.shape, 0)
    return jnp.concatenate([jnp.where(row == h, weight, 0.0) for h in range(heads)], axis=1)


def pack_kernel(keys, values, packed, sems):
    length = keys.shape[0]
    copies = [
        pltpu.make_async_copy(keys, packed.at[:length], sems.at[0]),
        pltpu.make_async_copy(values, packed.at[length:], sems.at[1]),
    ]
    for copy in copies:
        copy.start()
    for copy in copies:
        copy.wait()


def stats_kernel(count, *refs):
    sources = refs[:7]
    query, grad, weight, stats, partial, output, norm, bias, chosen, sems = refs[7:]
    copies = [
        pltpu.make_async_copy(source, target, sems.at[i])
        for i, (source, target) in enumerate(
            zip(sources, (weight, norm, bias, chosen, query, grad, output), strict=True)
        )
    ]
    for copy in copies:
        copy.start()
    for copy in copies[:4]:
        copy.wait()
    heads, head_dim = weight.shape
    length = query.shape[0]
    local = length // BLK
    rank = lax.axis_index("ctx")
    listed = chosen[...]
    lane_block = lax.broadcasted_iota(jnp.int32, (1, length), 1) // BLK
    for d in range(count):
        for b in range(local):
            block = lax.rem(rank - d + count, count) * local + b
            hit = jnp.max(jnp.where(listed == block, 1.0, 0.0), axis=1, keepdims=True)
            one = jnp.zeros((1, length), jnp.float32)
            for at in range(local):
                one = jnp.where(lane_block == at, (1.0 - hit[at : at + 1]) * OUT, one)
            at = 3 * heads + d * local + b
            stats[at : at + 1] = one
    eye = (
        lax.broadcasted_iota(jnp.int32, (heads, heads), 0)
        == lax.broadcasted_iota(jnp.int32, (heads, heads), 1)
    ).astype(jnp.float32)
    bias_col = jnp.sum(eye * bias[...], axis=1, keepdims=True)
    weight_high, weight_low = split16(head_blocks(weight[...]))
    ones = head_blocks(jnp.ones((heads, head_dim), jnp.float32)).astype(jnp.bfloat16)
    copies[4].wait()
    both = dot32(jnp.concatenate([weight_high, weight_low], axis=0), query[...], NT)
    logit = both[:heads] + both[heads:] + bias_col
    gate = jax.nn.sigmoid(logit)
    softplus = jnp.maximum(-logit, 0.0) + jnp.log1p(jnp.exp(-jnp.abs(logit)))
    stats[0:heads] = LOG2E * (norm[...] + softplus)
    copies[5].wait()
    copies[6].wait()
    product = grad[...].astype(jnp.float32) * output[...].astype(jnp.float32)
    high, low = split16(product)
    inner = dot32(ones, high, NT) + dot32(ones, low, NT)
    pre_grad = inner * gate * (1.0 - gate)
    stats[heads : 2 * heads] = inner
    stats[2 * heads : 3 * heads] = pre_grad
    pre_high, pre_low = split16(pre_grad)
    wide = dot32(jnp.concatenate([pre_high, pre_low], axis=0), query[...])
    wide = wide[:heads] + wide[heads:]
    for h in range(heads):
        partial[h : h + 1, :] = wide[h : h + 1, h * head_dim : (h + 1) * head_dim]
    total = jnp.sum(pre_grad, axis=1, keepdims=True)
    lane = lax.broadcasted_iota(jnp.int32, (heads, head_dim), 1)
    row = lax.broadcasted_iota(jnp.int32, (heads, head_dim), 0)
    partial[heads : heads + 8, :] = jnp.broadcast_to(
        jnp.sum(jnp.where(lane == row, total, 0.0), axis=0, keepdims=True), (8, head_dim)
    )


def final_kernel(count, parts_count, *refs):
    kv = refs[:count]
    parts = refs[count : count + parts_count]
    key_grad, value_grad, weight_grad, bias_grad = refs[count + parts_count :]
    length = key_grad.shape[0]
    heads = weight_grad.shape[0]
    total = functools.reduce(jnp.add, [ref[...] for ref in parts])
    weight_grad[...] = total[:heads]
    bias_grad[...] = total[heads : heads + 1, :heads]
    total = functools.reduce(jnp.add, [ref[...].astype(jnp.float32) for ref in kv])
    total = total.astype(jnp.bfloat16)
    key_grad[...] = total[:length]
    value_grad[...] = total[length:]


def attention_kernel(count, *refs):
    query, grad, stats, weight = refs[:4]
    kv = refs[4 : 4 + count]
    query_grad = refs[4 + count]
    kv_grad = refs[5 + count :]
    heads, head_dim = weight.shape
    length = query.shape[0]
    local = length // BLK
    factor = head_dim ** (-0.5)
    section = lax.axis_index("section")

    @pl.when(section == 0)
    def _():
        query_grad[...] = jnp.zeros_like(query_grad)
        for ref in kv_grad:
            ref[...] = jnp.zeros_like(ref)

    @pl.when(section > 0)
    def _():
        keys = jnp.concatenate([ref[:length] for ref in kv], axis=0)
        values = jnp.concatenate([ref[length:] for ref in kv], axis=0)
        keys_t = keys.T
        outs = [
            jnp.broadcast_to(stats[3 * heads + i : 3 * heads + i + 1], (BLK, length))
            for i in range(count * local)
        ]
        later = lax.broadcasted_iota(jnp.int32, (length, length), 0) > lax.broadcasted_iota(
            jnp.int32, (length, length), 1
        )
        own = jnp.where(later, OUT, jnp.concatenate(outs[:local], axis=0))
        masked = jnp.concatenate([own] + outs[local:], axis=0)
        masked = jnp.concatenate([masked, masked], axis=1)
        weight_high, weight_low = split16(head_blocks(weight[...]))
        pre_high, pre_low = split16(stats[2 * heads : 3 * heads])
        gate_term = dot32(
            jnp.concatenate([pre_high, pre_low, pre_high], axis=0),
            jnp.concatenate([weight_high, weight_high, weight_low], axis=0),
            TN,
        )
        key_acc = jnp.zeros((count * length, head_dim), jnp.float32)
        value_acc = jnp.zeros((count * length, head_dim), jnp.float32)
        for h in range(0, heads, 2):
            first = slice(h * head_dim, (h + 1) * head_dim)
            second = slice((h + 1) * head_dim, (h + 2) * head_dim)
            query_p = jnp.concatenate([query[:, first], query[:, second]], axis=0)
            grad_p = jnp.concatenate([grad[:, first], grad[:, second]], axis=0)
            norm_p = jnp.concatenate([stats[h : h + 1], stats[h + 1 : h + 2]], axis=1)
            inner_p = jnp.concatenate(
                [stats[heads + h : heads + h + 1], stats[heads + h + 1 : heads + h + 2]], axis=1
            )
            scores = dot32(keys, query_p, NT)
            raw = dot32(values, grad_p, NT)
            probs = jnp.exp2(scores * (factor * LOG2E) - (masked + norm_p))
            dscores = (probs * (raw - inner_p)).astype(jnp.bfloat16)
            value_acc += dot32(probs.astype(jnp.bfloat16), grad_p)
            key_acc += dot32(dscores, query_p)
            turned = dot32(keys_t, dscores).T
            query_grad[:, first] = (factor * turned[:length] + gate_term[:, first]).astype(
                jnp.bfloat16
            )
            query_grad[:, second] = (factor * turned[length:] + gate_term[:, second]).astype(
                jnp.bfloat16
            )
        for d, ref in enumerate(kv_grad):
            rows = slice(d * length, (d + 1) * length)
            ref[:length] = (factor * key_acc[rows]).astype(jnp.bfloat16)
            ref[length:] = value_acc[rows].astype(jnp.bfloat16)


def up_route(sections, size, d):
    route = {}
    for r in range(size):
        for s in range(2, sections):
            route[s, r] = (s, (r + d) % size)
        if sections > 1:
            route[1, r] = (1, r + d) if r + d < size else (0, r)
        if sections > 1:
            route[0, r] = (0, r - d) if r >= d else (1, r)
        else:
            route[0, r] = (0, r)
    return [(s * size + r, t * size + q) for (s, r), (t, q) in sorted(route.items())]


def down_route(sections, size, d):
    route = {}
    for r in range(size):
        for s in range(1, sections):
            if r >= d:
                route[s, r] = (s - 1, r - d)
    taken = set(route.values())
    if sections == 2 and d:
        for a in range(size - d):
            if a == size - 1 - d:
                for u in range(a, size - 1):
                    route[0, u] = (0, u + 1)
                route[0, size - 1] = (1, size - 1)
            elif a < d:
                route[0, a] = (1, a)
                route[1, a] = (1, a + d)
            else:
                route[0, a] = (1, a + d)
        for r in range(size):
            for s in range(2):
                route.setdefault((s, r), (s, r))
    else:
        free = [(s, r) for s in range(sections) for r in range(size) if (s, r) not in route]
        ends = [(s, r) for s in range(sections) for r in range(size) if (s, r) not in taken]
        route.update(zip(free, ends[-len(free) :], strict=True))
    return [(s * size + r, t * size + q) for (s, r), (t, q) in sorted(route.items())]


def shifted(array, axis):
    size = lax.axis_size(axis)
    return [
        lax.ppermute(array, axis, [(i, (i + d) % size) for i in range(size)])
        for d in range(1, size)
    ]


def on_device(
    queries, key_rows, value_rows, out_grad, attn_out, log_norm, selected, gate_weight, gate_bias
):
    length, width = queries.shape[2:]
    _, heads, head_dim = gate_weight.shape
    size = lax.axis_size("ctx")
    sections = lax.axis_size("section")
    local = length // BLK
    both_axes = ("section", "ctx")
    dma = pltpu.SemaphoreType.DMA
    hbm = pl.BlockSpec(memory_space=pltpu.HBM)
    vmem = pl.BlockSpec(memory_space=pltpu.VMEM)
    params = pltpu.CompilerParams(vmem_limit_bytes=VMEM_BYTES)

    def in_hbm(array):
        return pltpu.with_memory_space_constraint(array, pltpu.HBM)

    def shape(*dims, dtype=jnp.float32):
        return jax.ShapeDtypeStruct(dims, dtype)

    own_kv = pl.pallas_call(
        pack_kernel,
        out_shape=shape(2 * length, head_dim, dtype=jnp.bfloat16),
        in_specs=[hbm, hbm],
        out_specs=vmem,
        scratch_shapes=[dma((2,))],
        compiler_params=params,
        name="pack_keys_values",
    )(in_hbm(key_rows[0, 0]), in_hbm(value_rows[0, 0]))
    kv = [own_kv]
    for d in range(1, size):
        kv.append(lax.ppermute(own_kv, both_axes, up_route(sections, size, d)))
    query, grad, weight, stats, partial = pl.pallas_call(
        functools.partial(stats_kernel, size),
        out_shape=(
            shape(length, width, dtype=jnp.bfloat16),
            shape(length, width, dtype=jnp.bfloat16),
            shape(heads, head_dim),
            shape(3 * heads + size * local, length),
            shape(heads + 8, head_dim),
        ),
        in_specs=[hbm] * 7,
        out_specs=(vmem,) * 5,
        scratch_shapes=[
            pltpu.VMEM((length, width), jnp.bfloat16),
            pltpu.VMEM((heads, length), jnp.float32),
            pltpu.VMEM((1, heads), jnp.float32),
            pltpu.VMEM(selected.shape[2:], jnp.int32),
            dma((7,)),
        ],
        compiler_params=params,
        cost_estimate=pl.CostEstimate(
            flops=8 * heads * length * width, transcendentals=0, bytes_accessed=6 * length * width
        ),
        name="gate_stats",
    )(
        *map(
            in_hbm,
            (
                gate_weight[0],
                log_norm[0, 0].T,
                gate_bias,
                selected[0, 0],
                queries[0, 0],
                out_grad[0, 0],
                attn_out[0, 0],
            ),
        )
    )
    partial, *kv = lax.optimization_barrier((partial, *kv))
    by_dp = shifted(partial, "dp")
    results = pl.pallas_call(
        functools.partial(attention_kernel, size),
        out_shape=(shape(length, width, dtype=jnp.bfloat16),)
        + (shape(2 * length, head_dim, dtype=jnp.bfloat16),) * size,
        compiler_params=params,
        cost_estimate=pl.CostEstimate(
            flops=10 * size * length * length * width,
            transcendentals=size * length * length * heads,
            bytes_accessed=6 * length * width,
        ),
        name="attention_grads",
    )(query, grad, stats, weight, *kv)
    *results, partial = lax.optimization_barrier(
        (*results, functools.reduce(jnp.add, by_dp, partial))
    )
    query_sent = lax.ppermute(
        results[0], "section", [(s, (s - 1) % sections) for s in range(sections)]
    )
    kv_parts = [
        lax.ppermute(part, both_axes, down_route(sections, size, d))
        for d, part in enumerate(results[1:])
    ]
    parts = [partial] + shifted(partial, "ctx")
    key_grad, value_grad, weight_grad, bias_grad = pl.pallas_call(
        functools.partial(final_kernel, size, len(parts)),
        out_shape=(
            shape(length, head_dim, dtype=jnp.bfloat16),
            shape(length, head_dim, dtype=jnp.bfloat16),
            shape(heads, head_dim),
            shape(1, heads),
        ),
        compiler_params=params,
        name="final_sums",
    )(*kv_parts, *parts)
    return (
        query_sent[None, None],
        key_grad[None, None],
        value_grad[None, None],
        weight_grad[None],
        bias_grad,
    )


def solution(mesh):
    rows = P("dp", "section", "ctx", None)
    return jax.shard_map(
        on_device,
        mesh=mesh,
        in_specs=(rows,) * 7 + (P("section", None, None), P("section", None)),
        out_specs=(rows,) * 3 + (P("section", None, None), P("section", None)),
        check_vma=False,
    )
```

time: 42.4 us -> 34.6 us (0.82)
  starting transfers between devices: 23.7 us -> 16.3 us
  local copies, waits for them, and re-layouts: 7.83 us -> 0.79 us
  waiting for transfers between devices: 8.75 us -> 12.6 us
  Pallas kernels: 0.96 us -> 3.95 us
    ppermute x13, starting transfers between devices: 21.9 us -> 16.3 us  [the longest x6 6.28 us: shifted(): lax.ppermute(array, axis, [(i, (i + d) % size) for i in range(size)])]
    unnamed x18 -> x1, local copies, waits for them, and re-layouts: 6.09 us -> 0.79 us
    ppermute x13, waiting for transfers between devices: 8.75 us -> 12.6 us  [the longest x6 6.83 us: shifted(): lax.ppermute(array, axis, [(i, (i + d) % size) for i in range(size)])]
    pallas_call x2 -> x4, Pallas kernels: 0.96 us -> 3.95 us  [the longest x1 2.43 us: on_device(): pl.pallas_call(functools.partial(stats_kernel, size), out_shape=(shape(le...]
    ppermute x1, starting transfers between devices: 1.79 us -> 0.01 us  [on_device(): lax.ppermute(results[0], 'section', [(s, (s - 1) % sections) for s in ran...]
    broadcast_in_dim x2 -> x0, local copies, waits for them, and re-layouts: 1.23 us -> none  [the longest x1 0.63 us: on_device(): kv_sent[None, None, :, head_dim:]]
    slice x1 -> x0, local copies, waits for them, and re-layouts: 0.51 us -> none  [on_device(): total[heads:heads + 1, :heads]]
  transfers between devices with their start and end apart: 14 -> 14, of which waited for: 8 -> 10; matrix products, arithmetic and copies ran while one was open for 4% -> 0% of each run, Pallas kernels for 0% -> 9%
where the time goes in v2:
time: 34.6 us; the launch traced here: 34.3 us
  starting transfers between devices  16.3 us (47%)
  waiting for transfers between devices  12.6 us (36%)
  Pallas kernels  3.95 us (11%)
  local copies, waits for them, and re-layouts  0.79 us (2%)
  between operations  0.7 us (2%)
    ppermute x6, waiting for transfers between devices, shifted(): lax.ppermute(array, axis, [(i, (i + d) % size) for i in range(size)])  6.83 us
    ppermute x6, starting transfers between devices, shifted(): lax.ppermute(array, axis, [(i, (i + d) % size) for i in range(size)])  6.28 us
    ppermute x4, starting transfers between devices, on_device(): lax.ppermute(part, both_axes, down_route(sections, size, d))  5.33 us
    ppermute x3, starting transfers between devices, on_device(): kv.append(lax.ppermute(own_kv, both_axes, up_route(sections, size, d)))  4.66 us
    ppermute x4, waiting for transfers between devices, on_device(): lax.ppermute(part, both_axes, down_route(sections, size, d))  3.93 us
    pallas_call x1, Pallas kernels, on_device(): pl.pallas_call(functools.partial(stats_kernel, size), out_shape=(shape(le...  2.43 us
    ppermute x3, waiting for transfers between devices, on_device(): kv.append(lax.ppermute(own_kv, both_axes, up_route(sections, size, d)))  1.82 us
    unnamed x1, local copies, waits for them, and re-layouts  0.79 us
  transfers between devices with their start and end apart: 14, of which 10 were waited for; matrix products, arithmetic and copies ran while one was open for 0% of the time, Pallas kernels for 9%

profile of v2, /device:TPU:0, one launch (start us, length us, event | category | flops | bytes accessed | tf_op | source)
XLA Modules:
  0.0 34.3 jit_solution(791148734035471410)
XLA Ops:
  0.6 0.8 %pack_keys_values.1.refs_4_ = bf16[256,128]{1,0:T(8,128)(2,1)S(1)} custom-call(bf16[128,128]{1,0:T(8,128)(2,1)} %bitcast.18, bf16[128,128]{1,0:T(8,128)(2,1)} %bitcast.19), custom_call_target="tpu_custom_call" | custom-call | tf_op jit(solution)/shard_map/pack_keys_values/pallas_call | solution.py:262
  1.4 0.5 %collective-permute-start.2 = (bf16[256,128]{1,0:T(8,128)(2,1)S(1)}, bf16[256,128]{1,0:T(8,128)(2,1)S(1)}, u32[]{:S(2)}, u32[]{:S(2)}) collective-permute-start(bf16[256,128]{1,0:T(8,128)(2,1)S(1)} %pack_keys_values.1.refs_4_), channel_id=1, source_target_pairs={{0,4},{1,5},{2,6},{3,0},{4,7},{5,1},{6,2},{7,3},{8,12},{9,13},{10,... | collective-permute-start | bytes 196616 | tf_op jit(solution)/shard_map/ppermute | solution.py:273
  1.9 4.1 %collective-permute-start.1 = (bf16[256,128]{1,0:T(8,128)(2,1)S(1)}, bf16[256,128]{1,0:T(8,128)(2,1)S(1)}, u32[]{:S(2)}, u32[]{:S(2)}) collective-permute-start(bf16[256,128]{1,0:T(8,128)(2,1)S(1)} %pack_keys_values.1.refs_4_), channel_id=1, source_target_pairs={{0,4},{1,5},{2,0},{3,1},{4,6},{5,7},{6,2},{7,3},{8,12},{9,13},{10,... | collective-permute-start | bytes 196616 | tf_op jit(solution)/shard_map/ppermute | solution.py:273
  6.1 0.0 collective-permute-start
  6.1 2.4 %gate_stats.1 = (bf16[128,2048]{1,0:T(8,128)(2,1)S(1)}, bf16[128,2048]{1,0:T(8,128)(2,1)S(1)}, f32[16,128]{1,0:T(8,128)S(1)}, f32[56,128]{1,0:T(8,128)S(1)}, f32[24,128]{1,0:T(8,128)S(1)}) custom-call(f32[16,128]{1,0:T(8,128)} %bitcast.20, f32[16,128]{1,0:T(8,128)} %bitcast.21, f32[1,16]{1,0:T(1,128)} %refs_2_.1, s32[2,16]{1,0:T(2,128)} %bitcast.22, ...), custom_call_target="tpu_custom_call" | custom-call | flops 33554432 | bytes 1572864 | tf_op jit(solution)/shard_map/gate_stats/pallas_call | solution.py:274
  8.5 0.3 %collective-permute-done.2.refs_7_ = bf16[256,128]{1,0:T(8,128)(2,1)S(1)} collective-permute-done((bf16[256,128]{1,0:T(8,128)(2,1)S(1)}, bf16[256,128]{1,0:T(8,128)(2,1)S(1)}, u32[]{:S(2)}, u32[]{:S(2)}) %collective-permute-start.2) | collective-permute-done | bytes 65568 | tf_op jit(solution)/shard_map/ppermute | solution.py:273
  8.9 0.0 collective-permute-done.1.refs_6_
  8.9 1.5 %collective-permute-done.refs_5_ = bf16[256,128]{1,0:T(8,128)(2,1)S(1)} collective-permute-done((bf16[256,128]{1,0:T(8,128)(2,1)S(1)}, bf16[256,128]{1,0:T(8,128)(2,1)S(1)}, u32[]{:S(2)}, u32[]{:S(2)}) %collective-permute-start) | collective-permute-done | bytes 65568 | tf_op jit(solution)/shard_map/ppermute | solution.py:273
  10.4 2.4 %collective-permute-start.5 = (f32[24,128]{1,0:T(8,128)S(1)}, f32[24,128]{1,0:T(8,128)S(1)}, u32[]{:S(2)}, u32[]{:S(2)}) collective-permute-start(f32[24,128]{1,0:T(8,128)S(1)} %get-tuple-element.44), channel_id=1, source_target_pairs={{0,24},{8,0},{16,8},{24,16},{1,25},{9,1},{17,9},{25,17},{2,26},{10... | collective-permute-start | bytes 36872 | tf_op jit(solution)/shard_map/ppermute | solution.py:237
  12.8 0.5 %collective-permute-start.4 = (f32[24,128]{1,0:T(8,128)S(1)}, f32[24,128]{1,0:T(8,128)S(1)}, u32[]{:S(2)}, u32[]{:S(2)}) collective-permute-start(f32[24,128]{1,0:T(8,128)S(1)} %get-tuple-element.44), channel_id=1, source_target_pairs={{0,16},{8,24},{16,0},{24,8},{1,17},{9,25},{17,1},{25,9},{2,18},{10... | collective-permute-start | bytes 36872 | tf_op jit(solution)/shard_map/ppermute | solution.py:237
  13.3 0.6 %collective-permute-start.3 = (f32[24,128]{1,0:T(8,128)S(1)}, f32[24,128]{1,0:T(8,128)S(1)}, u32[]{:S(2)}, u32[]{:S(2)}) collective-permute-start(f32[24,128]{1,0:T(8,128)S(1)} %get-tuple-element.44), channel_id=1, source_target_pairs={{0,8},{8,16},{16,24},{24,0},{1,9},{9,17},{17,25},{25,1},{2,10},{10... | collective-permute-start | bytes 36872 | tf_op jit(solution)/shard_map/ppermute | solution.py:237
  13.9 0.1 attention_grads.1
  14.0 0.2 collective-permute-done.5
  14.2 2.3 %collective-permute-done.4 = f32[24,128]{1,0:T(8,128)S(1)} collective-permute-done((f32[24,128]{1,0:T(8,128)S(1)}, f32[24,128]{1,0:T(8,128)S(1)}, u32[]{:S(2)}, u32[]{:S(2)}) %collective-permute-start.4) | collective-permute-done | bytes 12320 | tf_op jit(solution)/shard_map/ppermute | solution.py:237
  16.5 1.4 %collective-permute-done.3 = f32[24,128]{1,0:T(8,128)S(1)} collective-permute-done((f32[24,128]{1,0:T(8,128)S(1)}, f32[24,128]{1,0:T(8,128)S(1)}, u32[]{:S(2)}, u32[]{:S(2)}) %collective-permute-start.3) | collective-permute-done | bytes 12320 | tf_op jit(solution)/shard_map/ppermute | solution.py:237
  17.9 0.0 collective-permute-start.6
  17.9 0.4 %collective-permute-start.13 = (f32[24,128]{1,0:T(8,128)S(1)}, f32[24,128]{1,0:T(8,128)S(1)}, u32[]{:S(2)}, u32[]{:S(2)}) collective-permute-start(f32[24,128]{1,0:T(8,128)S(1)} %add_add_fusion.refs_4_), channel_id=1, source_target_pairs={{0,3},{1,0},{2,1},{3,2},{4,7},{5,4},{6,5},{7,6},{8,11},{9,8},{10,9... | collective-permute-start | bytes 36872 | tf_op jit(solution)/shard_map/ppermute | solution.py:237
  18.3 1.6 %collective-permute-start.12 = (f32[24,128]{1,0:T(8,128)S(1)}, f32[24,128]{1,0:T(8,128)S(1)}, u32[]{:S(2)}, u32[]{:S(2)}) collective-permute-start(f32[24,128]{1,0:T(8,128)S(1)} %add_add_fusion.refs_4_), channel_id=1, source_target_pairs={{0,2},{1,3},{2,0},{3,1},{4,6},{5,7},{6,4},{7,5},{8,10},{9,11},{10,... | collective-permute-start | bytes 36872 | tf_op jit(solution)/shard_map/ppermute | solution.py:237
  19.9 0.7 %collective-permute-start.11 = (f32[24,128]{1,0:T(8,128)S(1)}, f32[24,128]{1,0:T(8,128)S(1)}, u32[]{:S(2)}, u32[]{:S(2)}) collective-permute-start(f32[24,128]{1,0:T(8,128)S(1)} %add_add_fusion.refs_4_), channel_id=1, source_target_pairs={{0,1},{1,2},{2,3},{3,0},{4,5},{5,6},{6,7},{7,4},{8,9},{9,10},{10,1... | collective-permute-start | bytes 36872 | tf_op jit(solution)/shard_map/ppermute | solution.py:237
  20.7 0.0 collective-permute-start.7
  20.7 1.0 %collective-permute-done.13.refs_7_ = f32[24,128]{1,0:T(8,128)S(1)} collective-permute-done((f32[24,128]{1,0:T(8,128)S(1)}, f32[24,128]{1,0:T(8,128)S(1)}, u32[]{:S(2)}, u32[]{:S(2)}) %collective-permute-start.13) | collective-permute-done | bytes 12320 | tf_op jit(solution)/shard_map/ppermute | solution.py:237
  21.7 0.0 collective-permute-start.8
  21.7 1.2 %collective-permute-done.12.refs_6_ = f32[24,128]{1,0:T(8,128)S(1)} collective-permute-done((f32[24,128]{1,0:T(8,128)S(1)}, f32[24,128]{1,0:T(8,128)S(1)}, u32[]{:S(2)}, u32[]{:S(2)}) %collective-permute-start.12) | collective-permute-done | bytes 12320 | tf_op jit(solution)/shard_map/ppermute | solution.py:237
  22.9 1.9 %collective-permute-start.9 = (bf16[256,128]{1,0:T(8,128)(2,1)S(1)}, bf16[256,128]{1,0:T(8,128)(2,1)S(1)}, u32[]{:S(2)}, u32[]{:S(2)}) collective-permute-start(bf16[256,128]{1,0:T(8,128)(2,1)S(1)} %get-tuple-element.48), channel_id=1, source_target_pairs={{0,4},{1,2},{2,3},{3,7},{4,6},{5,5},{6,0},{7,1},{8,12},{9,10},{10,... | collective-permute-start | bytes 196616 | tf_op jit(solution)/shard_map/ppermute | solution.py:332
  24.8 0.7 %collective-permute-done.11.refs_5_ = f32[24,128]{1,0:T(8,128)S(1)} collective-permute-done((f32[24,128]{1,0:T(8,128)S(1)}, f32[24,128]{1,0:T(8,128)S(1)}, u32[]{:S(2)}, u32[]{:S(2)}) %collective-permute-start.11) | collective-permute-done | bytes 12320 | tf_op jit(solution)/shard_map/ppermute | solution.py:237
  25.5 3.4 %collective-permute-start.10 = (bf16[256,128]{1,0:T(8,128)(2,1)S(1)}, bf16[256,128]{1,0:T(8,128)(2,1)S(1)}, u32[]{:S(2)}, u32[]{:S(2)}) collective-permute-start(bf16[256,128]{1,0:T(8,128)(2,1)S(1)} %get-tuple-element.49), channel_id=1, source_target_pairs={{0,1},{1,2},{2,3},{3,7},{4,4},{5,5},{6,6},{7,0},{8,9},{9,10},{10,1... | collective-permute-start | bytes 196616 | tf_op jit(solution)/shard_map/ppermute | solution.py:332
  28.9 0.0 collective-permute-done.7.refs_0_
  28.9 0.0 collective-permute-done.8.refs_1_
  28.9 0.5 %collective-permute-done.9.refs_2_ = bf16[256,128]{1,0:T(8,128)(2,1)S(1)} collective-permute-done((bf16[256,128]{1,0:T(8,128)(2,1)S(1)}, bf16[256,128]{1,0:T(8,128)(2,1)S(1)}, u32[]{:S(2)}, u32[]{:S(2)}) %collective-permute-start.9) | collective-permute-done | bytes 65568 | tf_op jit(solution)/shard_map/ppermute | solution.py:332
  29.4 3.5 %collective-permute-done.10.refs_3_ = bf16[256,128]{1,0:T(8,128)(2,1)S(1)} collective-permute-done((bf16[256,128]{1,0:T(8,128)(2,1)S(1)}, bf16[256,128]{1,0:T(8,128)(2,1)S(1)}, u32[]{:S(2)}, u32[]{:S(2)}) %collective-permute-start.10) | collective-permute-done | bytes 65568 | tf_op jit(solution)/shard_map/ppermute | solution.py:332
  32.9 0.7 %final_sums.1 = (bf16[128,128]{1,0:T(8,128)(2,1)}, bf16[128,128]{1,0:T(8,128)(2,1)}, f32[16,128]{1,0:T(8,128)}, f32[1,16]{1,0:T(1,128)}) custom-call(bf16[256,128]{1,0:T(8,128)(2,1)S(1)} %collective-permute-done.7.refs_0_, bf16[256,128]{1,0:T(8,128)(2,1)S(1)} %collective-permute-done.8.refs_1_, bf16[256,128]{1,0:T(8,128)(2,1)S(1)} %collective-permute-done.9.refs_2_, ...), custom_call_target="tpu_custom_call" | custom-call | tf_op jit(solution)/shard_map/final_sums/pallas_call | solution.py:336
  33.5 0.0 collective-permute-done.6
  33.5 0.8 %copy.15 = bf16[1,1,128,2048]{3,2,1,0:T(8,128)(2,1)} copy(bf16[1,1,128,2048]{3,2,1,0:T(8,128)(2,1)S(1)} %bitcast.17) | data formatting | bytes 1048576
  (1 shorter events, 0.0 us)
Async XLA Ops:
  1.4 7.5 %collective-permute-start.2 = (bf16[256,128]{1,0:T(8,128)(2,1)S(1)}, bf16[256,128]{1,0:T(8,128)(2,1)S(1)}, u32[]{:S(2)}, u32[]{:S(2)}) collective-permute-start(bf16[256,128]{1,0:T(8,128)(2,1)S(1)} %pack_keys_values.1.refs_4_), channel_id=1, source_target_pairs={{0,4},{1,5},{2,6},{3,0},{4,7},{5,1},{6,2},{7,3},{8,12},{9,13},{10,... | collective-permute-start | bytes 196616 | tf_op jit(solution)/shard_map/ppermute | solution.py:273
  1.9 6.9 %collective-permute-start.1 = (bf16[256,128]{1,0:T(8,128)(2,1)S(1)}, bf16[256,128]{1,0:T(8,128)(2,1)S(1)}, u32[]{:S(2)}, u32[]{:S(2)}) collective-permute-start(bf16[256,128]{1,0:T(8,128)(2,1)S(1)} %pack_keys_values.1.refs_4_), channel_id=1, source_target_pairs={{0,4},{1,5},{2,0},{3,1},{4,6},{5,7},{6,2},{7,3},{8,12},{9,13},{10,... | collective-permute-start | bytes 196616 | tf_op jit(solution)/shard_map/ppermute | solution.py:273
  6.1 4.3 %collective-permute-start = (bf16[256,128]{1,0:T(8,128)(2,1)S(1)}, bf16[256,128]{1,0:T(8,128)(2,1)S(1)}, u32[]{:S(2)}, u32[]{:S(2)}) collective-permute-start(bf16[256,128]{1,0:T(8,128)(2,1)S(1)} %pack_keys_values.1.refs_4_), channel_id=1, source_target_pairs={{0,4},{1,0},{2,1},{3,2},{4,5},{5,6},{6,7},{7,3},{8,12},{9,8},{10,9... | collective-permute-start | bytes 196616 | tf_op jit(solution)/shard_map/ppermute | solution.py:273
  10.4 3.9 %collective-permute-start.5 = (f32[24,128]{1,0:T(8,128)S(1)}, f32[24,128]{1,0:T(8,128)S(1)}, u32[]{:S(2)}, u32[]{:S(2)}) collective-permute-start(f32[24,128]{1,0:T(8,128)S(1)} %get-tuple-element.44), channel_id=1, source_target_pairs={{0,24},{8,0},{16,8},{24,16},{1,25},{9,1},{17,9},{25,17},{2,26},{10... | collective-permute-start | bytes 36872 | tf_op jit(solution)/shard_map/ppermute | solution.py:237
  12.8 3.7 %collective-permute-start.4 = (f32[24,128]{1,0:T(8,128)S(1)}, f32[24,128]{1,0:T(8,128)S(1)}, u32[]{:S(2)}, u32[]{:S(2)}) collective-permute-start(f32[24,128]{1,0:T(8,128)S(1)} %get-tuple-element.44), channel_id=1, source_target_pairs={{0,16},{8,24},{16,0},{24,8},{1,17},{9,25},{17,1},{25,9},{2,18},{10... | collective-permute-start | bytes 36872 | tf_op jit(solution)/shard_map/ppermute | solution.py:237
  13.3 4.6 %collective-permute-start.3 = (f32[24,128]{1,0:T(8,128)S(1)}, f32[24,128]{1,0:T(8,128)S(1)}, u32[]{:S(2)}, u32[]{:S(2)}) collective-permute-start(f32[24,128]{1,0:T(8,128)S(1)} %get-tuple-element.44), channel_id=1, source_target_pairs={{0,8},{8,16},{16,24},{24,0},{1,9},{9,17},{17,25},{25,1},{2,10},{10... | collective-permute-start | bytes 36872 | tf_op jit(solution)/shard_map/ppermute | solution.py:237
  17.9 15.6 %collective-permute-start.6 = (bf16[128,2048]{1,0:T(8,128)(2,1)S(1)}, bf16[128,2048]{1,0:T(8,128)(2,1)S(1)}, u32[]{:S(2)}, u32[]{:S(2)}) collective-permute-start(bf16[128,2048]{1,0:T(8,128)(2,1)S(1)} %get-tuple-element.45), channel_id=1, source_target_pairs={{0,4},{4,0},{1,5},{5,1},{2,6},{6,2},{3,7},{7,3},{8,12},{12,8},{9,1... | collective-permute-start | bytes 1572872 | tf_op jit(solution)/shard_map/ppermute | solution.py:328
  17.9 3.7 %collective-permute-start.13 = (f32[24,128]{1,0:T(8,128)S(1)}, f32[24,128]{1,0:T(8,128)S(1)}, u32[]{:S(2)}, u32[]{:S(2)}) collective-permute-start(f32[24,128]{1,0:T(8,128)S(1)} %add_add_fusion.refs_4_), channel_id=1, source_target_pairs={{0,3},{1,0},{2,1},{3,2},{4,7},{5,4},{6,5},{7,6},{8,11},{9,8},{10,9... | collective-permute-start | bytes 36872 | tf_op jit(solution)/shard_map/ppermute | solution.py:237
  18.3 4.6 %collective-permute-start.12 = (f32[24,128]{1,0:T(8,128)S(1)}, f32[24,128]{1,0:T(8,128)S(1)}, u32[]{:S(2)}, u32[]{:S(2)}) collective-permute-start(f32[24,128]{1,0:T(8,128)S(1)} %add_add_fusion.refs_4_), channel_id=1, source_target_pairs={{0,2},{1,3},{2,0},{3,1},{4,6},{5,7},{6,4},{7,5},{8,10},{9,11},{10,... | collective-permute-start | bytes 36872 | tf_op jit(solution)/shard_map/ppermute | solution.py:237
  19.9 5.6 %collective-permute-start.11 = (f32[24,128]{1,0:T(8,128)S(1)}, f32[24,128]{1,0:T(8,128)S(1)}, u32[]{:S(2)}, u32[]{:S(2)}) collective-permute-start(f32[24,128]{1,0:T(8,128)S(1)} %add_add_fusion.refs_4_), channel_id=1, source_target_pairs={{0,1},{1,2},{2,3},{3,0},{4,5},{5,6},{6,7},{7,4},{8,9},{9,10},{10,1... | collective-permute-start | bytes 36872 | tf_op jit(solution)/shard_map/ppermute | solution.py:237
  20.7 8.3 %collective-permute-start.7 = (bf16[256,128]{1,0:T(8,128)(2,1)S(1)}, bf16[256,128]{1,0:T(8,128)(2,1)S(1)}, u32[]{:S(2)}, u32[]{:S(2)}) collective-permute-start(bf16[256,128]{1,0:T(8,128)(2,1)S(1)} %get-tuple-element.46), channel_id=1, source_target_pairs={{0,4},{1,5},{2,6},{3,7},{4,0},{5,1},{6,2},{7,3},{8,12},{9,13},{10,... | collective-permute-start | bytes 196616 | tf_op jit(solution)/shard_map/ppermute | solution.py:332
  21.7 7.3 %collective-permute-start.8 = (bf16[256,128]{1,0:T(8,128)(2,1)S(1)}, bf16[256,128]{1,0:T(8,128)(2,1)S(1)}, u32[]{:S(2)}, u32[]{:S(2)}) collective-permute-start(bf16[256,128]{1,0:T(8,128)(2,1)S(1)} %get-tuple-element.47), channel_id=1, source_target_pairs={{0,4},{1,6},{2,3},{3,7},{4,5},{5,0},{6,1},{7,2},{8,12},{9,14},{10,... | collective-permute-start | bytes 196616 | tf_op jit(solution)/shard_map/ppermute | solution.py:332
  22.9 6.5 %collective-permute-start.9 = (bf16[256,128]{1,0:T(8,128)(2,1)S(1)}, bf16[256,128]{1,0:T(8,128)(2,1)S(1)}, u32[]{:S(2)}, u32[]{:S(2)}) collective-permute-start(bf16[256,128]{1,0:T(8,128)(2,1)S(1)} %get-tuple-element.48), channel_id=1, source_target_pairs={{0,4},{1,2},{2,3},{3,7},{4,6},{5,5},{6,0},{7,1},{8,12},{9,10},{10,... | collective-permute-start | bytes 196616 | tf_op jit(solution)/shard_map/ppermute | solution.py:332
  25.5 7.4 %collective-permute-start.10 = (bf16[256,128]{1,0:T(8,128)(2,1)S(1)}, bf16[256,128]{1,0:T(8,128)(2,1)S(1)}, u32[]{:S(2)}, u32[]{:S(2)}) collective-permute-start(bf16[256,128]{1,0:T(8,128)(2,1)S(1)} %get-tuple-element.49), channel_id=1, source_target_pairs={{0,1},{1,2},{2,3},{3,7},{4,4},{5,5},{6,6},{7,0},{8,9},{9,10},{10,1... | collective-permute-start | bytes 196616 | tf_op jit(solution)/shard_map/ppermute | solution.py:332

commit v3 on v2

v3 whole, which is shorter than its diff:
```python
import functools

import jax
import jax.numpy as jnp
from jax import lax
from jax.experimental import pallas as pl
from jax.experimental.pallas import tpu as pltpu
from jax.sharding import PartitionSpec as P

BLK = 64
FINAL_COST = 10000000000
QUERY_COST = 10000000000
OUT = 1e30
LOG2E = 1.4426950408889634
NT = (((1,), (1,)), ((), ()))
TN = (((0,), (0,)), ((), ()))
VMEM_BYTES = 24 * 1024 * 1024


def dot32(a, b, dims=(((1,), (0,)), ((), ())), precision=None):
    return lax.dot_general(a, b, dims, precision=precision, preferred_element_type=jnp.float32)


def split16(x):
    high = x.astype(jnp.bfloat16)
    low = (x - high.astype(jnp.float32)).astype(jnp.bfloat16)
    return high, low


def head_blocks(weight):
    heads = weight.shape[0]
    row = lax.broadcasted_iota(jnp.int32, weight.shape, 0)
    return jnp.concatenate([jnp.where(row == h, weight, 0.0) for h in range(heads)], axis=1)


def load_kernel(*refs):
    keys, values, *sources = refs[:9]
    packed, *targets, sems = refs[9:]
    length = keys.shape[0]
    copies = [
        pltpu.make_async_copy(source, target, sems.at[i])
        for i, (source, target) in enumerate(
            zip(
                (keys, values, *sources),
                (packed.at[:length], packed.at[length:], *targets),
                strict=True,
            )
        )
    ]
    for copy in copies:
        copy.start()
    for copy in copies:
        copy.wait()


def stats_kernel(count, *refs):
    weight, norm, bias, chosen, query, grad, output, stats, partial = refs
    heads, head_dim = weight.shape
    length = query.shape[0]
    local = length // BLK
    rank = lax.axis_index("ctx")
    listed = chosen[...]
    lane_block = lax.broadcasted_iota(jnp.int32, (1, length), 1) // BLK
    for d in range(count):
        for b in range(local):
            block = lax.rem(rank - d + count, count) * local + b
            hit = jnp.max(jnp.where(listed == block, 1.0, 0.0), axis=1, keepdims=True)
            one = jnp.zeros((1, length), jnp.float32)
            for at in range(local):
                one = jnp.where(lane_block == at, (1.0 - hit[at : at + 1]) * OUT, one)
            at = 3 * heads + d * local + b
            stats[at : at + 1] = one
    eye = (
        lax.broadcasted_iota(jnp.int32, (heads, heads), 0)
        == lax.broadcasted_iota(jnp.int32, (heads, heads), 1)
    ).astype(jnp.float32)
    bias_col = jnp.sum(eye * bias[...], axis=1, keepdims=True)
    weight_high, weight_low = split16(head_blocks(weight[...]))
    ones = head_blocks(jnp.ones((heads, head_dim), jnp.float32)).astype(jnp.bfloat16)
    both = dot32(jnp.concatenate([weight_high, weight_low], axis=0), query[...], NT)
    logit = both[:heads] + both[heads:] + bias_col
    gate = jax.nn.sigmoid(logit)
    softplus = jnp.maximum(-logit, 0.0) + jnp.log1p(jnp.exp(-jnp.abs(logit)))
    stats[0:heads] = LOG2E * (norm[...] + softplus)
    product = grad[...].astype(jnp.float32) * output[...].astype(jnp.float32)
    high, low = split16(product)
    inner = dot32(ones, high, NT) + dot32(ones, low, NT)
    pre_grad = inner * gate * (1.0 - gate)
    stats[heads : 2 * heads] = inner
    stats[2 * heads : 3 * heads] = pre_grad
    pre_high, pre_low = split16(pre_grad)
    wide = dot32(jnp.concatenate([pre_high, pre_low], axis=0), query[...])
    wide = wide[:heads] + wide[heads:]
    total = jnp.sum(pre_grad, axis=1, keepdims=True)
    lane = lax.broadcasted_iota(jnp.int32, (heads, head_dim), 1)
    row = lax.broadcasted_iota(jnp.int32, (heads, head_dim), 0)
    bias_row = jnp.sum(jnp.where(lane == row, total, 0.0), axis=0, keepdims=True)
    one = jnp.zeros((heads, head_dim), jnp.float32)
    for h in range(heads):
        one += jnp.where(row == h, wide[:, h * head_dim : (h + 1) * head_dim], 0.0)
    bias_rows = jnp.broadcast_to(bias_row, (8, head_dim))
    for i in range(partial.shape[0]):
        partial[i, :heads] = one
        partial[i, heads:] = bias_rows


def final_kernel(*refs):
    *kv, parts, key_grad, value_grad, weight_grad, bias_grad = refs
    length = key_grad.shape[0]
    heads = weight_grad.shape[0]
    total = jnp.sum(parts[...], axis=0)
    weight_grad[...] = total[:heads]
    bias_grad[...] = total[heads : heads + 1, :heads]
    total = functools.reduce(jnp.add, [ref[...].astype(jnp.float32) for ref in kv])
    total = total.astype(jnp.bfloat16)
    key_grad[...] = total[:length]
    value_grad[...] = total[length:]


def scores_kernel(count, *refs):
    query, grad, stats = refs[:3]
    kv = refs[3 : 3 + count]
    dscores_out = refs[3 + count]
    kv_grad = refs[4 + count :]
    length = query.shape[0]
    head_dim = kv[0].shape[1]
    heads = query.shape[1] // head_dim
    local = length // BLK
    factor = head_dim ** (-0.5)
    section = lax.axis_index("section")

    @pl.when(section == 0)
    def _():
        for ref in kv_grad:
            ref[...] = jnp.zeros_like(ref)

    @pl.when(section > 0)
    def _():
        keys = jnp.concatenate([ref[:length] for ref in kv], axis=0)
        values = jnp.concatenate([ref[length:] for ref in kv], axis=0)
        outs = [
            jnp.broadcast_to(stats[3 * heads + i : 3 * heads + i + 1], (BLK, length))
            for i in range(count * local)
        ]
        later = lax.broadcasted_iota(jnp.int32, (length, length), 0) > lax.broadcasted_iota(
            jnp.int32, (length, length), 1
        )
        own = jnp.where(later, OUT, jnp.concatenate(outs[:local], axis=0))
        masked = jnp.concatenate([own] + outs[local:], axis=0)
        masked = jnp.concatenate([masked, masked], axis=1)
        key_acc = jnp.zeros((count * length, head_dim), jnp.float32)
        value_acc = jnp.zeros((count * length, head_dim), jnp.float32)
        for h in range(0, heads, 2):
            first = slice(h * head_dim, (h + 1) * head_dim)
            second = slice((h + 1) * head_dim, (h + 2) * head_dim)
            query_p = jnp.concatenate([query[:, first], query[:, second]], axis=0)
            grad_p = jnp.concatenate([grad[:, first], grad[:, second]], axis=0)
            norm_p = jnp.concatenate([stats[h : h + 1], stats[h + 1 : h + 2]], axis=1)
            inner_p = jnp.concatenate(
                [stats[heads + h : heads + h + 1], stats[heads + h + 1 : heads + h + 2]], axis=1
            )
            scores = dot32(keys, query_p, NT)
            raw = dot32(values, grad_p, NT)
            probs = jnp.exp2(scores * (factor * LOG2E) - (masked + norm_p))
            dscores = (probs * (raw - inner_p)).astype(jnp.bfloat16)
            value_acc += dot32(probs.astype(jnp.bfloat16), grad_p)
            key_acc += dot32(dscores, query_p)
            dscores_out[:, h * length : (h + 2) * length] = dscores
        for d, ref in enumerate(kv_grad):
            rows = slice(d * length, (d + 1) * length)
            ref[:length] = (factor * key_acc[rows]).astype(jnp.bfloat16)
            ref[length:] = value_acc[rows].astype(jnp.bfloat16)


def query_kernel(count, *refs):
    dscores, stats, weight = refs[:3]
    kv = refs[3 : 3 + count]
    packed = refs[3 + count]
    heads, head_dim = weight.shape
    length = packed.shape[0]
    factor = head_dim ** (-0.5)
    section = lax.axis_index("section")

    @pl.when(section == 0)
    def _():
        packed[...] = jnp.zeros_like(packed)

    @pl.when(section > 0)
    def _():
        keys_t = jnp.concatenate([ref[:length] for ref in kv], axis=0).T
        weight_high, weight_low = split16(head_blocks(weight[...]))
        pre_high, pre_low = split16(stats[2 * heads : 3 * heads])
        gate_term = dot32(
            jnp.concatenate([pre_high, pre_low, pre_high], axis=0),
            jnp.concatenate([weight_high, weight_high, weight_low], axis=0),
            TN,
        )
        for h in range(0, heads, 2):
            turned = dot32(keys_t, dscores[:, h * length : (h + 2) * length]).T
            for at in range(2):
                columns = slice((h + at) * head_dim, (h + at + 1) * head_dim)
                packed[:, columns] = (
                    factor * turned[at * length : (at + 1) * length] + gate_term[:, columns]
                ).astype(jnp.bfloat16)


def up_route(sections, size, d):
    route = {}
    for r in range(size):
        for s in range(2, sections):
            route[s, r] = (s, (r + d) % size)
        if sections > 1:
            route[1, r] = (1, r + d) if r + d < size else (0, r)
        if sections > 1:
            route[0, r] = (0, r - d) if r >= d else (1, r)
        else:
            route[0, r] = (0, r)
    return [(s * size + r, t * size + q) for (s, r), (t, q) in sorted(route.items())]


def down_route(sections, size, d):
    route = [
        (s * size + r, (s - 1) * size + r - d) for s in range(1, sections) for r in range(d, size)
    ]
    if d == 0:
        route += [(r, (sections - 1) * size + r) for r in range(size)]
    return route


def on_device(
    queries, key_rows, value_rows, out_grad, attn_out, log_norm, selected, gate_weight, gate_bias
):
    length, width = queries.shape[2:]
    _, heads, head_dim = gate_weight.shape
    size = lax.axis_size("ctx")
    sections = lax.axis_size("section")
    local = length // BLK
    both_axes = ("section", "ctx")
    dma = pltpu.SemaphoreType.DMA
    hbm = pl.BlockSpec(memory_space=pltpu.HBM)
    vmem = pl.BlockSpec(memory_space=pltpu.VMEM)
    params = pltpu.CompilerParams(vmem_limit_bytes=VMEM_BYTES)

    def in_hbm(array):
        return pltpu.with_memory_space_constraint(array, pltpu.HBM)

    def shape(*dims, dtype=jnp.float32):
        return jax.ShapeDtypeStruct(dims, dtype)

    sources = (
        gate_weight[0],
        log_norm[0, 0].T,
        gate_bias,
        selected[0, 0],
        queries[0, 0],
        out_grad[0, 0],
        attn_out[0, 0],
    )
    own_kv, *loaded = pl.pallas_call(
        load_kernel,
        out_shape=(shape(2 * length, head_dim, dtype=jnp.bfloat16),)
        + tuple(shape(*source.shape, dtype=source.dtype) for source in sources),
        in_specs=[hbm] * 9,
        out_specs=(vmem,) * 8,
        scratch_shapes=[dma((9,))],
        compiler_params=params,
        name="load",
    )(*map(in_hbm, (key_rows[0, 0], value_rows[0, 0], *sources)))
    weight, query, grad = loaded[0], loaded[4], loaded[5]
    kv = [own_kv]
    for d in range(1, size):
        kv.append(lax.ppermute(own_kv, both_axes, up_route(sections, size, d)))
    stats, partial = pl.pallas_call(
        functools.partial(stats_kernel, size),
        out_shape=(
            shape(3 * heads + size * local, length),
            shape(size * lax.axis_size("dp"), heads + 8, head_dim),
        ),
        compiler_params=params,
        cost_estimate=pl.CostEstimate(
            flops=8 * heads * length * width, transcendentals=0, bytes_accessed=6 * length * width
        ),
        name="gate_stats",
    )(*loaded)
    partial, kv[1:2] = lax.optimization_barrier((partial, kv[1:2]))
    partial = lax.all_to_all(partial, ("dp", "ctx"), 0, 0)
    dscores, *kv_grad = pl.pallas_call(
        functools.partial(scores_kernel, size),
        out_shape=(shape(size * length, heads * length, dtype=jnp.bfloat16),)
        + (shape(2 * length, head_dim, dtype=jnp.bfloat16),) * size,
        compiler_params=params,
        cost_estimate=pl.CostEstimate(
            flops=8 * size * length * length * width,
            transcendentals=size * length * length * heads,
            bytes_accessed=6 * length * width,
        ),
        name="score_grads",
    )(query, grad, stats, *kv)
    kv_parts = [
        lax.ppermute(kv_grad[d], both_axes, down_route(sections, size, d)) for d in range(size)
    ]
    packed = pl.pallas_call(
        functools.partial(query_kernel, size),
        out_shape=shape(length, width, dtype=jnp.bfloat16),
        compiler_params=params,
        cost_estimate=pl.CostEstimate(
            flops=QUERY_COST,
            transcendentals=0,
            bytes_accessed=6 * length * width,
        ),
        name="query_grads",
    )(dscores, stats, weight, *kv)
    query_sent = lax.ppermute(
        packed, "section", [(s, (s - 1) % sections) for s in range(sections)]
    )
    key_grad, value_grad, weight_grad, bias_grad = pl.pallas_call(
        final_kernel,
        out_shape=(
            shape(length, head_dim, dtype=jnp.bfloat16),
            shape(length, head_dim, dtype=jnp.bfloat16),
            shape(heads, head_dim),
            shape(1, heads),
        ),
        compiler_params=params,
        cost_estimate=pl.CostEstimate(
            flops=FINAL_COST, transcendentals=0, bytes_accessed=4 * length * width
        ),
        name="final_sums",
    )(*kv_parts[::-1], partial)
    return (
        query_sent[None, None],
        key_grad[None, None],
        value_grad[None, None],
        weight_grad[None],
        bias_grad,
    )


def solution(mesh):
    rows = P("dp", "section", "ctx", None)
    return jax.shard_map(
        on_device,
        mesh=mesh,
        in_specs=(rows,) * 7 + (P("section", None, None), P("section", None)),
        out_specs=(rows,) * 3 + (P("section", None, None), P("section", None)),
        check_vma=False,
    )
```

time: 34.6 us -> 24.9 us (0.72)
  waiting for transfers between devices: 12.6 us -> 4.01 us
  starting transfers between devices: 16.3 us -> 15.2 us
    ppermute x11 -> x5, waiting for transfers between devices: 10.8 us -> 4 us  [the longest x4 4 us: on_device(): lax.ppermute(kv_grad[d], both_axes, down_route(sections, size, d))]
    ppermute x11 -> x5, starting transfers between devices: 11.6 us -> 5.16 us  [the longest x4 3.95 us: on_device(): lax.ppermute(kv_grad[d], both_axes, down_route(sections, size, d))]
    all_to_all x0 -> x1, starting transfers between devices: none -> 4.74 us  [on_device(): partial = lax.all_to_all(partial, ('dp', 'ctx'), 0, 0)]
    ppermute x3, waiting for transfers between devices: 1.82 us -> 0.01 us  [on_device(): kv.append(lax.ppermute(own_kv, both_axes, up_route(sections, size, d)))]
    ppermute x3, starting transfers between devices: 4.66 us -> 5.3 us  [on_device(): kv.append(lax.ppermute(own_kv, both_axes, up_route(sections, size, d)))]
    pallas_call x4 -> x5, Pallas kernels: 3.95 us -> 3.86 us  [the longest x1 1.55 us: on_device(): pl.pallas_call(functools.partial(stats_kernel, size), out_shape=(shape(3...]
  transfers between devices with their start and end apart: 14 -> 9, of which waited for: 10 -> 3; matrix products, arithmetic and copies ran while one was open for 0% -> 0% of each run, Pallas kernels for 9% -> 9%
where the time goes in v3:
time: 24.9 us; the launch traced here: 24.6 us
  starting transfers between devices  15.2 us (61%)
  waiting for transfers between devices  4.01 us (16%)
  Pallas kernels  3.86 us (16%)
  local copies, waits for them, and re-layouts  0.79 us (3%)
  between operations  0.72 us (3%)
    ppermute x3, starting transfers between devices, on_device(): kv.append(lax.ppermute(own_kv, both_axes, up_route(sections, size, d)))  5.3 us
    all_to_all x1, starting transfers between devices, on_device(): partial = lax.all_to_all(partial, ('dp', 'ctx'), 0, 0)  4.74 us
    ppermute x4, waiting for transfers between devices, on_device(): lax.ppermute(kv_grad[d], both_axes, down_route(sections, size, d))  4 us
    ppermute x4, starting transfers between devices, on_device(): lax.ppermute(kv_grad[d], both_axes, down_route(sections, size, d))  3.95 us
    pallas_call x1, Pallas kernels, on_device(): pl.pallas_call(functools.partial(stats_kernel, size), out_shape=(shape(3...  1.55 us
    pallas_call x1, Pallas kernels, on_device(): pl.pallas_call(load_kernel, out_shape=(shape(2 * length, head_dim, dtype=...  1.55 us
    ppermute x1, starting transfers between devices, on_device(): lax.ppermute(packed, 'section', [(s, (s - 1) % sections) for s in range(s...  1.21 us
    unnamed x1, local copies, waits for them, and re-layouts  0.79 us
  transfers between devices with their start and end apart: 9, of which 3 were waited for; matrix products, arithmetic and copies ran while one was open for 0% of the time, Pallas kernels for 9%

profile of v3, /device:TPU:0, one launch (start us, length us, event | category | flops | bytes accessed | tf_op | source)
XLA Modules:
  0.0 24.6 jit_solution(1716620151669440488)
XLA Ops:
  0.6 1.5 %load.1 = (bf16[256,128]{1,0:T(8,128)(2,1)S(1)}, f32[16,128]{1,0:T(8,128)S(1)}, f32[16,128]{1,0:T(8,128)S(1)}, f32[1,16]{1,0:T(1,128)S(1)}, s32[2,16]{1,0:T(2,12...) custom-call(bf16[128,128]{1,0:T(8,128)(2,1)} %bitcast.18, ...), custom_call_target="tpu_custom_call" | custom-call | tf_op jit(solution)/shard_map/load/pallas_call | solution.py:259
  2.2 0.5 %collective-permute-start = (bf16[256,128]{1,0:T(8,128)(2,1)S(1)}, bf16[256,128]{1,0:T(8,128)(2,1)S(1)}, u32[]{:S(2)}, u32[]{:S(2)}) collective-permute-start(bf16[256,128]{1,0:T(8,128)(2,1)S(1)} %get-tuple-element.34.refs_3_), channel_id=1, source_target_pairs={{0,4},{1,0},{2,1},{3,2},{4,5},{5,6},{6,7},{7,3},{8,12},{9,8},{10,9... | collective-permute-start | bytes 196616 | tf_op jit(solution)/shard_map/ppermute | solution.py:272
  2.7 2.1 %collective-permute-start.2 = (bf16[256,128]{1,0:T(8,128)(2,1)S(1)}, bf16[256,128]{1,0:T(8,128)(2,1)S(1)}, u32[]{:S(2)}, u32[]{:S(2)}) collective-permute-start(bf16[256,128]{1,0:T(8,128)(2,1)S(1)} %get-tuple-element.34.refs_3_), channel_id=1, source_target_pairs={{0,4},{1,5},{2,6},{3,0},{4,7},{5,1},{6,2},{7,3},{8,12},{9,13},{10,... | collective-permute-start | bytes 196616 | tf_op jit(solution)/shard_map/ppermute | solution.py:272
  4.8 2.7 %collective-permute-start.1 = (bf16[256,128]{1,0:T(8,128)(2,1)S(1)}, bf16[256,128]{1,0:T(8,128)(2,1)S(1)}, u32[]{:S(2)}, u32[]{:S(2)}) collective-permute-start(bf16[256,128]{1,0:T(8,128)(2,1)S(1)} %get-tuple-element.34.refs_3_), channel_id=1, source_target_pairs={{0,4},{1,5},{2,0},{3,1},{4,6},{5,7},{6,2},{7,3},{8,12},{9,13},{10,... | collective-permute-start | bytes 196616 | tf_op jit(solution)/shard_map/ppermute | solution.py:272
  7.5 1.5 %gate_stats.1 = (f32[56,128]{1,0:T(8,128)S(1)}, f32[16,24,128]{2,1,0:T(8,128)}) custom-call(f32[16,128]{1,0:T(8,128)S(1)} %get-tuple-element.28.refs_0_.refs_2_, f32[16,128]{1,0:T(8,128)S(1)} %get-tuple-element.29.refs_1_, f32[1,16]{1,0:T(1,128)S(1)} %get-tuple-element.30.refs_2_, s32[2,16]{1,0:T(2,128)S(1)} %get-tuple-element.31.refs_3_, ...), custom_call_target="tpu_custom_call" | custom-call | flops 33554432 | bytes 1572864 | tf_op jit(solution)/shard_map/gate_stats/pallas_call | solution.py:273
  9.0 0.0 collective-permute-done.refs_4_
  9.0 4.7 %all-to-all-start = ((f32[16,24,128]{2,1,0:T(8,128)}), f32[16,24,128]{2,1,0:T(8,128)S(1)}, u32[]{:S(2)}, u32[]{:S(2)}) async-start(f32[16,24,128]{2,1,0:T(8,128)} %get-tuple-element.42), calls=%async_computation | async-start | bytes 393216 | tf_op jit(solution)/shard_map/all_to_all | solution.py:286
  13.8 0.0 collective-permute-done.2.refs_6_
  13.8 0.0 collective-permute-done.1.refs_5_
  13.8 0.1 score_grads.1
  13.9 1.3 %collective-permute-start.4 = (bf16[256,128]{1,0:T(8,128)(2,1)S(1)}, bf16[256,128]{1,0:T(8,128)(2,1)S(1)}, u32[]{:S(2)}, u32[]{:S(2)}) collective-permute-start(bf16[256,128]{1,0:T(8,128)(2,1)S(1)} %get-tuple-element.38), channel_id=1, source_target_pairs={{7,0},{15,8},{23,16},{31,24}} | collective-permute-start | bytes 196616 | tf_op jit(solution)/shard_map/ppermute | solution.py:300
  15.2 1.3 %collective-permute-start.5 = (bf16[256,128]{1,0:T(8,128)(2,1)S(1)}, bf16[256,128]{1,0:T(8,128)(2,1)S(1)}, u32[]{:S(2)}, u32[]{:S(2)}) collective-permute-start(bf16[256,128]{1,0:T(8,128)(2,1)S(1)} %get-tuple-element.39), channel_id=1, source_target_pairs={{6,0},{7,1},{14,8},{15,9},{22,16},{23,17},{30,24},{31,25}} | collective-permute-start | bytes 196616 | tf_op jit(solution)/shard_map/ppermute | solution.py:300
  16.5 1.3 %collective-permute-start.6 = (bf16[256,128]{1,0:T(8,128)(2,1)S(1)}, bf16[256,128]{1,0:T(8,128)(2,1)S(1)}, u32[]{:S(2)}, u32[]{:S(2)}) collective-permute-start(bf16[256,128]{1,0:T(8,128)(2,1)S(1)} %get-tuple-element.40), channel_id=1, source_target_pairs={{5,0},{6,1},{7,2},{13,8},{14,9},{15,10},{21,16},{22,17},{23,18},{2... | collective-permute-start | bytes 196616 | tf_op jit(solution)/shard_map/ppermute | solution.py:300
  17.8 0.1 collective-permute-start.7
  17.8 0.1 query_grads.1
  17.9 1.2 %collective-permute-start.3 = (bf16[128,2048]{1,0:T(8,128)(2,1)S(1)}, bf16[128,2048]{1,0:T(8,128)(2,1)S(1)}, u32[]{:S(2)}, u32[]{:S(2)}) collective-permute-start(bf16[128,2048]{1,0:T(8,128)(2,1)S(1)} %query_grads.1), channel_id=1, source_target_pairs={{0,4},{4,0},{1,5},{5,1},{2,6},{6,2},{3,7},{7,3},{8,12},{12,8},{9,1... | collective-permute-start | bytes 1572872 | tf_op jit(solution)/shard_map/ppermute | solution.py:313
  19.1 2.8 %collective-permute-done.4.refs_0_ = bf16[256,128]{1,0:T(8,128)(2,1)S(1)} collective-permute-done((bf16[256,128]{1,0:T(8,128)(2,1)S(1)}, bf16[256,128]{1,0:T(8,128)(2,1)S(1)}, u32[]{:S(2)}, u32[]{:S(2)}) %collective-permute-start.4) | collective-permute-done | bytes 65568 | tf_op jit(solution)/shard_map/ppermute | solution.py:300
  21.9 0.6 %collective-permute-done.5.refs_1_ = bf16[256,128]{1,0:T(8,128)(2,1)S(1)} collective-permute-done((bf16[256,128]{1,0:T(8,128)(2,1)S(1)}, bf16[256,128]{1,0:T(8,128)(2,1)S(1)}, u32[]{:S(2)}, u32[]{:S(2)}) %collective-permute-start.5) | collective-permute-done | bytes 65568 | tf_op jit(solution)/shard_map/ppermute | solution.py:300
  22.5 0.6 %collective-permute-done.6.refs_2_ = bf16[256,128]{1,0:T(8,128)(2,1)S(1)} collective-permute-done((bf16[256,128]{1,0:T(8,128)(2,1)S(1)}, bf16[256,128]{1,0:T(8,128)(2,1)S(1)}, u32[]{:S(2)}, u32[]{:S(2)}) %collective-permute-start.6) | collective-permute-done | bytes 65568 | tf_op jit(solution)/shard_map/ppermute | solution.py:300
  23.1 0.0 collective-permute-done.7.refs_3_
  23.1 0.0 all-to-all-done.refs_4_
  23.1 0.7 %final_sums.1 = (bf16[128,128]{1,0:T(8,128)(2,1)}, bf16[128,128]{1,0:T(8,128)(2,1)}, f32[16,128]{1,0:T(8,128)}, f32[1,16]{1,0:T(1,128)}) custom-call(bf16[256,128]{1,0:T(8,128)(2,1)S(1)} %collective-permute-done.4.refs_0_, bf16[256,128]{1,0:T(8,128)(2,1)S(1)} %collective-permute-done.5.refs_1_, bf16[256,128]{1,0:T(8,128)(2,1)S(1)} %collective-permute-done.6.refs_2_, ...), custom_call_target="tpu_custom_call" | custom-call | flops 10000000000 | bytes 1048576 | tf_op jit(solution)/shard_map/final_sums/pallas_call | solution.py:316
  23.8 0.0 collective-permute-done.3
  23.8 0.8 %copy.15 = bf16[1,1,128,2048]{3,2,1,0:T(8,128)(2,1)} copy(bf16[1,1,128,2048]{3,2,1,0:T(8,128)(2,1)S(1)} %bitcast.17) | data formatting | bytes 1048576
Async XLA Ops:
  2.2 6.8 %collective-permute-start = (bf16[256,128]{1,0:T(8,128)(2,1)S(1)}, bf16[256,128]{1,0:T(8,128)(2,1)S(1)}, u32[]{:S(2)}, u32[]{:S(2)}) collective-permute-start(bf16[256,128]{1,0:T(8,128)(2,1)S(1)} %get-tuple-element.34.refs_3_), channel_id=1, source_target_pairs={{0,4},{1,0},{2,1},{3,2},{4,5},{5,6},{6,7},{7,3},{8,12},{9,8},{10,9... | collective-permute-start | bytes 196616 | tf_op jit(solution)/shard_map/ppermute | solution.py:272
  2.7 11.1 %collective-permute-start.2 = (bf16[256,128]{1,0:T(8,128)(2,1)S(1)}, bf16[256,128]{1,0:T(8,128)(2,1)S(1)}, u32[]{:S(2)}, u32[]{:S(2)}) collective-permute-start(bf16[256,128]{1,0:T(8,128)(2,1)S(1)} %get-tuple-element.34.refs_3_), channel_id=1, source_target_pairs={{0,4},{1,5},{2,6},{3,0},{4,7},{5,1},{6,2},{7,3},{8,12},{9,13},{10,... | collective-permute-start | bytes 196616 | tf_op jit(solution)/shard_map/ppermute | solution.py:272
  4.8 9.0 %collective-permute-start.1 = (bf16[256,128]{1,0:T(8,128)(2,1)S(1)}, bf16[256,128]{1,0:T(8,128)(2,1)S(1)}, u32[]{:S(2)}, u32[]{:S(2)}) collective-permute-start(bf16[256,128]{1,0:T(8,128)(2,1)S(1)} %get-tuple-element.34.refs_3_), channel_id=1, source_target_pairs={{0,4},{1,5},{2,0},{3,1},{4,6},{5,7},{6,2},{7,3},{8,12},{9,13},{10,... | collective-permute-start | bytes 196616 | tf_op jit(solution)/shard_map/ppermute | solution.py:272
  9.0 14.1 %all-to-all-start = ((f32[16,24,128]{2,1,0:T(8,128)}), f32[16,24,128]{2,1,0:T(8,128)S(1)}, u32[]{:S(2)}, u32[]{:S(2)}) async-start(f32[16,24,128]{2,1,0:T(8,128)} %get-tuple-element.42), calls=%async_computation | async-start | bytes 393216 | tf_op jit(solution)/shard_map/all_to_all | solution.py:286
  13.9 8.1 %collective-permute-start.4 = (bf16[256,128]{1,0:T(8,128)(2,1)S(1)}, bf16[256,128]{1,0:T(8,128)(2,1)S(1)}, u32[]{:S(2)}, u32[]{:S(2)}) collective-permute-start(bf16[256,128]{1,0:T(8,128)(2,1)S(1)} %get-tuple-element.38), channel_id=1, source_target_pairs={{7,0},{15,8},{23,16},{31,24}} | collective-permute-start | bytes 196616 | tf_op jit(solution)/shard_map/ppermute | solution.py:300
  15.2 7.4 %collective-permute-start.5 = (bf16[256,128]{1,0:T(8,128)(2,1)S(1)}, bf16[256,128]{1,0:T(8,128)(2,1)S(1)}, u32[]{:S(2)}, u32[]{:S(2)}) collective-permute-start(bf16[256,128]{1,0:T(8,128)(2,1)S(1)} %get-tuple-element.39), channel_id=1, source_target_pairs={{6,0},{7,1},{14,8},{15,9},{22,16},{23,17},{30,24},{31,25}} | collective-permute-start | bytes 196616 | tf_op jit(solution)/shard_map/ppermute | solution.py:300
  16.5 6.7 %collective-permute-start.6 = (bf16[256,128]{1,0:T(8,128)(2,1)S(1)}, bf16[256,128]{1,0:T(8,128)(2,1)S(1)}, u32[]{:S(2)}, u32[]{:S(2)}) collective-permute-start(bf16[256,128]{1,0:T(8,128)(2,1)S(1)} %get-tuple-element.40), channel_id=1, source_target_pairs={{5,0},{6,1},{7,2},{13,8},{14,9},{15,10},{21,16},{22,17},{23,18},{2... | collective-permute-start | bytes 196616 | tf_op jit(solution)/shard_map/ppermute | solution.py:300
  17.8 5.4 %collective-permute-start.7 = (bf16[256,128]{1,0:T(8,128)(2,1)S(1)}, bf16[256,128]{1,0:T(8,128)(2,1)S(1)}, u32[]{:S(2)}, u32[]{:S(2)}) collective-permute-start(bf16[256,128]{1,0:T(8,128)(2,1)S(1)} %get-tuple-element.41), channel_id=1, source_target_pairs={{4,0},{5,1},{6,2},{7,3},{0,4},{1,5},{2,6},{3,7},{12,8},{13,9},{14,... | collective-permute-start | bytes 196616 | tf_op jit(solution)/shard_map/ppermute | solution.py:300
  17.9 5.9 %collective-permute-start.3 = (bf16[128,2048]{1,0:T(8,128)(2,1)S(1)}, bf16[128,2048]{1,0:T(8,128)(2,1)S(1)}, u32[]{:S(2)}, u32[]{:S(2)}) collective-permute-start(bf16[128,2048]{1,0:T(8,128)(2,1)S(1)} %query_grads.1), channel_id=1, source_target_pairs={{0,4},{4,0},{1,5},{5,1},{2,6},{6,2},{3,7},{7,3},{8,12},{12,8},{9,1... | collective-permute-start | bytes 1572872 | tf_op jit(solution)/shard_map/ppermute | solution.py:313

commit v4 on v3

--- a/solution.py
+++ b/solution.py
@@ -105,16 +105,35 @@
 
 
 def final_kernel(*refs):
-    *kv, parts, key_grad, value_grad, weight_grad, bias_grad = refs
+    *kv, parts, kv_total, gate_total = refs
+    gate_total[...] = jnp.sum(parts[...], axis=0)
+    total = functools.reduce(jnp.add, [ref[...].astype(jnp.float32) for ref in kv])
+    kv_total[...] = total.astype(jnp.bfloat16)
+
+
+def output_kernel(query, kv_total, gate_total, *refs):
+    query_grad, key_grad, value_grad, weight_grad, bias_grad, bias, sems = refs
     length = key_grad.shape[0]
     heads = weight_grad.shape[0]
-    total = jnp.sum(parts[...], axis=0)
-    weight_grad[...] = total[:heads]
-    bias_grad[...] = total[heads : heads + 1, :heads]
-    total = functools.reduce(jnp.add, [ref[...].astype(jnp.float32) for ref in kv])
-    total = total.astype(jnp.bfloat16)
-    key_grad[...] = total[:length]
-    value_grad[...] = total[length:]
+    copies = [
+        pltpu.make_async_copy(source, target, sems.at[i])
+        for i, (source, target) in enumerate(
+            (
+                (query.at[: length // 2], query_grad.at[: length // 2]),
+                (query.at[length // 2 :], query_grad.at[length // 2 :]),
+                (kv_total.at[:length], key_grad),
+                (kv_total.at[length:], value_grad),
+                (gate_total.at[:heads], weight_grad),
+                (bias, bias_grad),
+            )
+        )
+    ]
+    for copy in copies[:-1]:
+        copy.start()
+    bias[...] = gate_total[heads : heads + 1, :heads]
+    copies[-1].start()
+    for copy in copies:
+        copy.wait()
 
 
 def scores_kernel(count, *refs):
@@ -282,7 +301,6 @@
         ),
         name="gate_stats",
     )(*loaded)
-    partial, kv[1:2] = lax.optimization_barrier((partial, kv[1:2]))
     partial = lax.all_to_all(partial, ("dp", "ctx"), 0, 0)
     dscores, *kv_grad = pl.pallas_call(
         functools.partial(scores_kernel, size),
@@ -313,22 +331,34 @@
     query_sent = lax.ppermute(
         packed, "section", [(s, (s - 1) % sections) for s in range(sections)]
     )
-    key_grad, value_grad, weight_grad, bias_grad = pl.pallas_call(
+    kv_total, gate_total = pl.pallas_call(
         final_kernel,
         out_shape=(
+            shape(2 * length, head_dim, dtype=jnp.bfloat16),
+            shape(heads + 8, head_dim),
+        ),
+        compiler_params=params,
+        cost_estimate=pl.CostEstimate(
+            flops=FINAL_COST, transcendentals=0, bytes_accessed=4 * length * width
+        ),
+        name="final_sums",
+    )(*kv_parts[::-1], partial)
+    query_grad, key_grad, value_grad, weight_grad, bias_grad = pl.pallas_call(
+        output_kernel,
+        out_shape=(
+            shape(length, width, dtype=jnp.bfloat16),
             shape(length, head_dim, dtype=jnp.bfloat16),
             shape(length, head_dim, dtype=jnp.bfloat16),
             shape(heads, head_dim),
             shape(1, heads),
         ),
-        compiler_params=params,
-        cost_estimate=pl.CostEstimate(
-            flops=FINAL_COST, transcendentals=0, bytes_accessed=4 * length * width
-        ),
-        name="final_sums",
-    )(*kv_parts[::-1], partial)
+        out_specs=(hbm,) * 5,
+        scratch_shapes=[pltpu.VMEM((1, heads), jnp.float32), dma((6,))],
+        compiler_params=params,
+        name="outputs",
+    )(query_sent, kv_total, gate_total)
     return (
-        query_sent[None, None],
+        query_grad[None, None],
         key_grad[None, None],
         value_grad[None, None],
         weight_grad[None],

time: 24.9 us -> 24.2 us (0.972)
  local copies, waits for them, and re-layouts: 0.79 us -> 0 us
  Pallas kernels: 3.86 us -> 4.11 us
    unnamed x1 -> x0, local copies, waits for them, and re-layouts: 0.79 us -> none
    ppermute x3, starting transfers between devices: 5.3 us -> 4.66 us  [on_device(): kv.append(lax.ppermute(own_kv, both_axes, up_route(sections, size, d)))]
    all_to_all x1, starting transfers between devices: 4.74 us -> 5.29 us  [on_device(): partial = lax.all_to_all(partial, ('dp', 'ctx'), 0, 0)]
    pallas_call x1 -> x2, Pallas kernels: 0.66 us -> 0.91 us  [the longest x1 0.86 us: on_device(): pl.pallas_call(output_kernel, out_shape=(shape(length, width, dtype=jnp.b...]
  transfers between devices with their start and end apart: 9 -> 9, of which waited for: 3 -> 3; matrix products, arithmetic and copies ran while one was open for 0% -> 0% of each run, Pallas kernels for 9% -> 7%
where the time goes in v4:
time: 24.2 us; the launch traced here: 23.9 us
  starting transfers between devices  15.1 us (62%)
  Pallas kernels  4.11 us (17%)
  waiting for transfers between devices  3.95 us (16%)
  between operations  0.74 us (3%)
    all_to_all x1, starting transfers between devices, on_device(): partial = lax.all_to_all(partial, ('dp', 'ctx'), 0, 0)  5.29 us
    ppermute x3, starting transfers between devices, on_device(): kv.append(lax.ppermute(own_kv, both_axes, up_route(sections, size, d)))  4.66 us
    ppermute x4, starting transfers between devices, on_device(): lax.ppermute(kv_grad[d], both_axes, down_route(sections, size, d))  3.95 us
    ppermute x4, waiting for transfers between devices, on_device(): lax.ppermute(kv_grad[d], both_axes, down_route(sections, size, d))  3.94 us
    pallas_call x1, Pallas kernels, on_device(): pl.pallas_call(functools.partial(stats_kernel, size), out_shape=(shape(3...  1.55 us
    pallas_call x1, Pallas kernels, on_device(): pl.pallas_call(load_kernel, out_shape=(shape(2 * length, head_dim, dtype=...  1.55 us
    ppermute x1, starting transfers between devices, on_device(): lax.ppermute(packed, 'section', [(s, (s - 1) % sections) for s in range(s...  1.21 us
    pallas_call x1, Pallas kernels, on_device(): pl.pallas_call(output_kernel, out_shape=(shape(length, width, dtype=jnp.b...  0.86 us
  transfers between devices with their start and end apart: 9, of which 3 were waited for; matrix products, arithmetic and copies ran while one was open for 0% of the time, Pallas kernels for 7%

profile of v4, /device:TPU:0, one launch (start us, length us, event | category | flops | bytes accessed | tf_op | source)
XLA Modules:
  0.0 23.9 jit_solution(6394013337346172520)
XLA Ops:
  0.6 1.5 %load.1 = (bf16[256,128]{1,0:T(8,128)(2,1)S(1)}, f32[16,128]{1,0:T(8,128)S(1)}, f32[16,128]{1,0:T(8,128)S(1)}, f32[1,16]{1,0:T(1,128)S(1)}, s32[2,16]{1,0:T(2,12...) custom-call(bf16[128,128]{1,0:T(8,128)(2,1)} %bitcast.17, ...), custom_call_target="tpu_custom_call" | custom-call | tf_op jit(solution)/shard_map/load/pallas_call | solution.py:278
  2.2 0.5 %collective-permute-start.2 = (bf16[256,128]{1,0:T(8,128)(2,1)S(1)}, bf16[256,128]{1,0:T(8,128)(2,1)S(1)}, u32[]{:S(2)}, u32[]{:S(2)}) collective-permute-start(bf16[256,128]{1,0:T(8,128)(2,1)S(1)} %get-tuple-element.35.refs_3_), channel_id=1, source_target_pairs={{0,4},{1,5},{2,6},{3,0},{4,7},{5,1},{6,2},{7,3},{8,12},{9,13},{10,... | collective-permute-start | bytes 196616 | tf_op jit(solution)/shard_map/ppermute | solution.py:291
  2.7 4.1 %collective-permute-start.1 = (bf16[256,128]{1,0:T(8,128)(2,1)S(1)}, bf16[256,128]{1,0:T(8,128)(2,1)S(1)}, u32[]{:S(2)}, u32[]{:S(2)}) collective-permute-start(bf16[256,128]{1,0:T(8,128)(2,1)S(1)} %get-tuple-element.35.refs_3_), channel_id=1, source_target_pairs={{0,4},{1,5},{2,0},{3,1},{4,6},{5,7},{6,2},{7,3},{8,12},{9,13},{10,... | collective-permute-start | bytes 196616 | tf_op jit(solution)/shard_map/ppermute | solution.py:291
  6.8 0.0 collective-permute-start
  6.8 1.5 %gate_stats.1 = (f32[56,128]{1,0:T(8,128)S(1)}, f32[16,24,128]{2,1,0:T(8,128)}) custom-call(f32[16,128]{1,0:T(8,128)S(1)} %get-tuple-element.29.refs_0_.refs_2_, f32[16,128]{1,0:T(8,128)S(1)} %get-tuple-element.30.refs_1_, f32[1,16]{1,0:T(1,128)S(1)} %get-tuple-element.31.refs_2_, s32[2,16]{1,0:T(2,128)S(1)} %get-tuple-element.32.refs_3_, ...), custom_call_target="tpu_custom_call" | custom-call | flops 33554432 | bytes 1572864 | tf_op jit(solution)/shard_map/gate_stats/pallas_call | solution.py:292
  8.4 5.3 %all-to-all-start = ((f32[16,24,128]{2,1,0:T(8,128)}), f32[16,24,128]{2,1,0:T(8,128)S(1)}, u32[]{:S(2)}, u32[]{:S(2)}) async-start(f32[16,24,128]{2,1,0:T(8,128)} %get-tuple-element.41), calls=%async_computation | async-start | bytes 393216 | tf_op jit(solution)/shard_map/all_to_all | solution.py:304
  13.7 0.0 collective-permute-done.2.refs_6_
  13.7 0.0 collective-permute-done.1.refs_5_
  13.7 0.0 collective-permute-done.refs_4_
  13.7 0.1 score_grads.1
  13.8 1.3 %collective-permute-start.4 = (bf16[256,128]{1,0:T(8,128)(2,1)S(1)}, bf16[256,128]{1,0:T(8,128)(2,1)S(1)}, u32[]{:S(2)}, u32[]{:S(2)}) collective-permute-start(bf16[256,128]{1,0:T(8,128)(2,1)S(1)} %get-tuple-element.37), channel_id=1, source_target_pairs={{7,0},{15,8},{23,16},{31,24}} | collective-permute-start | bytes 196616 | tf_op jit(solution)/shard_map/ppermute | solution.py:318
  15.1 1.3 %collective-permute-start.5 = (bf16[256,128]{1,0:T(8,128)(2,1)S(1)}, bf16[256,128]{1,0:T(8,128)(2,1)S(1)}, u32[]{:S(2)}, u32[]{:S(2)}) collective-permute-start(bf16[256,128]{1,0:T(8,128)(2,1)S(1)} %get-tuple-element.38), channel_id=1, source_target_pairs={{6,0},{7,1},{14,8},{15,9},{22,16},{23,17},{30,24},{31,25}} | collective-permute-start | bytes 196616 | tf_op jit(solution)/shard_map/ppermute | solution.py:318
  16.4 1.3 %collective-permute-start.6 = (bf16[256,128]{1,0:T(8,128)(2,1)S(1)}, bf16[256,128]{1,0:T(8,128)(2,1)S(1)}, u32[]{:S(2)}, u32[]{:S(2)}) collective-permute-start(bf16[256,128]{1,0:T(8,128)(2,1)S(1)} %get-tuple-element.39), channel_id=1, source_target_pairs={{5,0},{6,1},{7,2},{13,8},{14,9},{15,10},{21,16},{22,17},{23,18},{2... | collective-permute-start | bytes 196616 | tf_op jit(solution)/shard_map/ppermute | solution.py:318
  17.7 0.1 collective-permute-start.7
  17.8 0.1 query_grads.1
  17.8 1.2 %collective-permute-start.3 = (bf16[128,2048]{1,0:T(8,128)(2,1)S(1)}, bf16[128,2048]{1,0:T(8,128)(2,1)S(1)}, u32[]{:S(2)}, u32[]{:S(2)}) collective-permute-start(bf16[128,2048]{1,0:T(8,128)(2,1)S(1)} %query_grads.1), channel_id=1, source_target_pairs={{0,4},{4,0},{1,5},{5,1},{2,6},{6,2},{3,7},{7,3},{8,12},{12,8},{9,1... | collective-permute-start | bytes 1572872 | tf_op jit(solution)/shard_map/ppermute | solution.py:331
  19.0 2.6 %collective-permute-done.4.refs_0_ = bf16[256,128]{1,0:T(8,128)(2,1)S(1)} collective-permute-done((bf16[256,128]{1,0:T(8,128)(2,1)S(1)}, bf16[256,128]{1,0:T(8,128)(2,1)S(1)}, u32[]{:S(2)}, u32[]{:S(2)}) %collective-permute-start.4) | collective-permute-done | bytes 65568 | tf_op jit(solution)/shard_map/ppermute | solution.py:318
  21.6 0.7 %collective-permute-done.5.refs_1_ = bf16[256,128]{1,0:T(8,128)(2,1)S(1)} collective-permute-done((bf16[256,128]{1,0:T(8,128)(2,1)S(1)}, bf16[256,128]{1,0:T(8,128)(2,1)S(1)}, u32[]{:S(2)}, u32[]{:S(2)}) %collective-permute-start.5) | collective-permute-done | bytes 65568 | tf_op jit(solution)/shard_map/ppermute | solution.py:318
  22.4 0.6 %collective-permute-done.6.refs_2_ = bf16[256,128]{1,0:T(8,128)(2,1)S(1)} collective-permute-done((bf16[256,128]{1,0:T(8,128)(2,1)S(1)}, bf16[256,128]{1,0:T(8,128)(2,1)S(1)}, u32[]{:S(2)}, u32[]{:S(2)}) %collective-permute-start.6) | collective-permute-done | bytes 65568 | tf_op jit(solution)/shard_map/ppermute | solution.py:318
  23.0 0.0 collective-permute-done.7.refs_3_
  23.0 0.0 all-to-all-done.refs_4_
  23.0 0.1 final_sums.1
  23.0 0.0 collective-permute-done.3.query
  23.0 0.9 %outputs.1 = (bf16[128,2048]{1,0:T(8,128)(2,1)}, bf16[128,128]{1,0:T(8,128)(2,1)}, bf16[128,128]{1,0:T(8,128)(2,1)}, f32[16,128]{1,0:T(8,128)}, f32[1,16]{1,0:T(1,128)}) custom-call(bf16[128,2048]{1,0:T(8,128)(2,1)S(1)} %collective-permute-done.3.query, bf16[256,128]{1,0:T(8,128)(2,1)S(1)} %get-tuple-element.42.kv_total, ...), custom_call_target="tpu_custom_call" | custom-call | tf_op jit(solution)/shard_map/outputs/pallas_call | solution.py:346
Async XLA Ops:
  2.2 11.5 %collective-permute-start.2 = (bf16[256,128]{1,0:T(8,128)(2,1)S(1)}, bf16[256,128]{1,0:T(8,128)(2,1)S(1)}, u32[]{:S(2)}, u32[]{:S(2)}) collective-permute-start(bf16[256,128]{1,0:T(8,128)(2,1)S(1)} %get-tuple-element.35.refs_3_), channel_id=1, source_target_pairs={{0,4},{1,5},{2,6},{3,0},{4,7},{5,1},{6,2},{7,3},{8,12},{9,13},{10,... | collective-permute-start | bytes 196616 | tf_op jit(solution)/shard_map/ppermute | solution.py:291
  2.7 11.0 %collective-permute-start.1 = (bf16[256,128]{1,0:T(8,128)(2,1)S(1)}, bf16[256,128]{1,0:T(8,128)(2,1)S(1)}, u32[]{:S(2)}, u32[]{:S(2)}) collective-permute-start(bf16[256,128]{1,0:T(8,128)(2,1)S(1)} %get-tuple-element.35.refs_3_), channel_id=1, source_target_pairs={{0,4},{1,5},{2,0},{3,1},{4,6},{5,7},{6,2},{7,3},{8,12},{9,13},{10,... | collective-permute-start | bytes 196616 | tf_op jit(solution)/shard_map/ppermute | solution.py:291
  6.8 6.9 %collective-permute-start = (bf16[256,128]{1,0:T(8,128)(2,1)S(1)}, bf16[256,128]{1,0:T(8,128)(2,1)S(1)}, u32[]{:S(2)}, u32[]{:S(2)}) collective-permute-start(bf16[256,128]{1,0:T(8,128)(2,1)S(1)} %get-tuple-element.35.refs_3_), channel_id=1, source_target_pairs={{0,4},{1,0},{2,1},{3,2},{4,5},{5,6},{6,7},{7,3},{8,12},{9,8},{10,9... | collective-permute-start | bytes 196616 | tf_op jit(solution)/shard_map/ppermute | solution.py:291
  8.4 14.6 %all-to-all-start = ((f32[16,24,128]{2,1,0:T(8,128)}), f32[16,24,128]{2,1,0:T(8,128)S(1)}, u32[]{:S(2)}, u32[]{:S(2)}) async-start(f32[16,24,128]{2,1,0:T(8,128)} %get-tuple-element.41), calls=%async_computation | async-start | bytes 393216 | tf_op jit(solution)/shard_map/all_to_all | solution.py:304
  13.8 7.9 %collective-permute-start.4 = (bf16[256,128]{1,0:T(8,128)(2,1)S(1)}, bf16[256,128]{1,0:T(8,128)(2,1)S(1)}, u32[]{:S(2)}, u32[]{:S(2)}) collective-permute-start(bf16[256,128]{1,0:T(8,128)(2,1)S(1)} %get-tuple-element.37), channel_id=1, source_target_pairs={{7,0},{15,8},{23,16},{31,24}} | collective-permute-start | bytes 196616 | tf_op jit(solution)/shard_map/ppermute | solution.py:318
  15.1 7.3 %collective-permute-start.5 = (bf16[256,128]{1,0:T(8,128)(2,1)S(1)}, bf16[256,128]{1,0:T(8,128)(2,1)S(1)}, u32[]{:S(2)}, u32[]{:S(2)}) collective-permute-start(bf16[256,128]{1,0:T(8,128)(2,1)S(1)} %get-tuple-element.38), channel_id=1, source_target_pairs={{6,0},{7,1},{14,8},{15,9},{22,16},{23,17},{30,24},{31,25}} | collective-permute-start | bytes 196616 | tf_op jit(solution)/shard_map/ppermute | solution.py:318
  16.4 6.6 %collective-permute-start.6 = (bf16[256,128]{1,0:T(8,128)(2,1)S(1)}, bf16[256,128]{1,0:T(8,128)(2,1)S(1)}, u32[]{:S(2)}, u32[]{:S(2)}) collective-permute-start(bf16[256,128]{1,0:T(8,128)(2,1)S(1)} %get-tuple-element.39), channel_id=1, source_target_pairs={{5,0},{6,1},{7,2},{13,8},{14,9},{15,10},{21,16},{22,17},{23,18},{2... | collective-permute-start | bytes 196616 | tf_op jit(solution)/shard_map/ppermute | solution.py:318
  17.7 5.3 %collective-permute-start.7 = (bf16[256,128]{1,0:T(8,128)(2,1)S(1)}, bf16[256,128]{1,0:T(8,128)(2,1)S(1)}, u32[]{:S(2)}, u32[]{:S(2)}) collective-permute-start(bf16[256,128]{1,0:T(8,128)(2,1)S(1)} %get-tuple-element.40), channel_id=1, source_target_pairs={{4,0},{5,1},{6,2},{7,3},{0,4},{1,5},{2,6},{3,7},{12,8},{13,9},{14,... | collective-permute-start | bytes 196616 | tf_op jit(solution)/shard_map/ppermute | solution.py:318
  17.8 5.2 %collective-permute-start.3 = (bf16[128,2048]{1,0:T(8,128)(2,1)S(1)}, bf16[128,2048]{1,0:T(8,128)(2,1)S(1)}, u32[]{:S(2)}, u32[]{:S(2)}) collective-permute-start(bf16[128,2048]{1,0:T(8,128)(2,1)S(1)} %query_grads.1), channel_id=1, source_target_pairs={{0,4},{4,0},{1,5},{5,1},{2,6},{6,2},{3,7},{7,3},{8,12},{12,8},{9,1... | collective-permute-start | bytes 1572872 | tf_op jit(solution)/shard_map/ppermute | solution.py:331

commit v5 on v4

--- a/solution.py
+++ b/solution.py
@@ -33,31 +33,32 @@
     return jnp.concatenate([jnp.where(row == h, weight, 0.0) for h in range(heads)], axis=1)
 
 
-def load_kernel(*refs):
-    keys, values, *sources = refs[:9]
-    packed, *targets, sems = refs[9:]
-    length = keys.shape[0]
+def prepare_kernel(count, *refs):
+    sources = refs[:9]
+    packed, weight, query, grad, stats, partial = refs[9:15]
+    norm, bias, chosen, output, sems = refs[15:]
+    heads, head_dim = weight.shape
+    length = query.shape[0]
+    local = length // BLK
+    targets = (
+        weight,
+        norm,
+        bias,
+        chosen,
+        query,
+        grad,
+        output,
+        packed.at[:length],
+        packed.at[length:],
+    )
     copies = [
         pltpu.make_async_copy(source, target, sems.at[i])
-        for i, (source, target) in enumerate(
-            zip(
-                (keys, values, *sources),
-                (packed.at[:length], packed.at[length:], *targets),
-                strict=True,
-            )
-        )
+        for i, (source, target) in enumerate(zip(sources, targets, strict=True))
     ]
     for copy in copies:
         copy.start()
-    for copy in copies:
+    for copy in copies[:4]:
         copy.wait()
-
-
-def stats_kernel(count, *refs):
-    weight, norm, bias, chosen, query, grad, output, stats, partial = refs
-    heads, head_dim = weight.shape
-    length = query.shape[0]
-    local = length // BLK
     rank = lax.axis_index("ctx")
     listed = chosen[...]
     lane_block = lax.broadcasted_iota(jnp.int32, (1, length), 1) // BLK
@@ -76,16 +77,25 @@
     ).astype(jnp.float32)
     bias_col = jnp.sum(eye * bias[...], axis=1, keepdims=True)
     weight_high, weight_low = split16(head_blocks(weight[...]))
-    ones = head_blocks(jnp.ones((heads, head_dim), jnp.float32)).astype(jnp.bfloat16)
+    width = heads * head_dim
+    indicator = (
+        lax.broadcasted_iota(jnp.int32, (width, heads), 0) // head_dim
+        == lax.broadcasted_iota(jnp.int32, (width, heads), 1)
+    ).astype(jnp.bfloat16)
+    copies[4].wait()
     both = dot32(jnp.concatenate([weight_high, weight_low], axis=0), query[...], NT)
     logit = both[:heads] + both[heads:] + bias_col
     gate = jax.nn.sigmoid(logit)
     softplus = jnp.maximum(-logit, 0.0) + jnp.log1p(jnp.exp(-jnp.abs(logit)))
     stats[0:heads] = LOG2E * (norm[...] + softplus)
+    slope = gate * (1.0 - gate)
+    copies[5].wait()
+    copies[6].wait()
     product = grad[...].astype(jnp.float32) * output[...].astype(jnp.float32)
     high, low = split16(product)
-    inner = dot32(ones, high, NT) + dot32(ones, low, NT)
-    pre_grad = inner * gate * (1.0 - gate)
+    sums = dot32(jnp.concatenate([high, low], axis=0), indicator)
+    inner = (sums[:length] + sums[length:]).T
+    pre_grad = inner * slope
     stats[heads : 2 * heads] = inner
     stats[2 * heads : 3 * heads] = pre_grad
     pre_high, pre_low = split16(pre_grad)
@@ -102,6 +112,8 @@
     for i in range(partial.shape[0]):
         partial[i, :heads] = one
         partial[i, heads:] = bias_rows
+    for copy in copies[7:]:
+        copy.wait()
 
 
 def final_kernel(*refs):
@@ -275,32 +287,34 @@
         out_grad[0, 0],
         attn_out[0, 0],
     )
-    own_kv, *loaded = pl.pallas_call(
-        load_kernel,
-        out_shape=(shape(2 * length, head_dim, dtype=jnp.bfloat16),)
-        + tuple(shape(*source.shape, dtype=source.dtype) for source in sources),
+    own_kv, weight, query, grad, stats, partial = pl.pallas_call(
+        functools.partial(prepare_kernel, size),
+        out_shape=(
+            shape(2 * length, head_dim, dtype=jnp.bfloat16),
+            shape(heads, head_dim),
+            shape(length, width, dtype=jnp.bfloat16),
+            shape(length, width, dtype=jnp.bfloat16),
+            shape(3 * heads + size * local, length),
+            shape(size * lax.axis_size("dp"), heads + 8, head_dim),
+        ),
         in_specs=[hbm] * 9,
-        out_specs=(vmem,) * 8,
-        scratch_shapes=[dma((9,))],
-        compiler_params=params,
-        name="load",
-    )(*map(in_hbm, (key_rows[0, 0], value_rows[0, 0], *sources)))
-    weight, query, grad = loaded[0], loaded[4], loaded[5]
+        out_specs=(vmem,) * 6,
+        scratch_shapes=[
+            pltpu.VMEM((heads, length), jnp.float32),
+            pltpu.VMEM((1, heads), jnp.float32),
+            pltpu.VMEM(selected.shape[2:], jnp.int32),
+            pltpu.VMEM((length, width), jnp.bfloat16),
+            dma((9,)),
+        ],
+        compiler_params=params,
+        cost_estimate=pl.CostEstimate(
+            flops=8 * heads * length * width, transcendentals=0, bytes_accessed=6 * length * width
+        ),
+        name="prepare",
+    )(*map(in_hbm, (*sources, key_rows[0, 0], value_rows[0, 0])))
     kv = [own_kv]
     for d in range(1, size):
         kv.append(lax.ppermute(own_kv, both_axes, up_route(sections, size, d)))
-    stats, partial = pl.pallas_call(
-        functools.partial(stats_kernel, size),
-        out_shape=(
-            shape(3 * heads + size * local, length),
-            shape(size * lax.axis_size("dp"), heads + 8, head_dim),
-        ),
-        compiler_params=params,
-        cost_estimate=pl.CostEstimate(
-            flops=8 * heads * length * width, transcendentals=0, bytes_accessed=6 * length * width
-        ),
-        name="gate_stats",
-    )(*loaded)
     partial = lax.all_to_all(partial, ("dp", "ctx"), 0, 0)
     dscores, *kv_grad = pl.pallas_call(
         functools.partial(scores_kernel, size),

time: 24.2 us -> 24 us (level)
  Pallas kernels: 4.11 us -> 3.86 us
    pallas_call x2 -> x1, Pallas kernels: 3.09 us -> 2.86 us  [on_device(): pl.pallas_call(functools.partial(prepare_kernel, size), out_shape=(shape(...]
  transfers between devices with their start and end apart: 9 -> 9, of which waited for: 3 -> 3; matrix products, arithmetic and copies ran while one was open for 0% -> 0% of each run, Pallas kernels for 7% -> 1%
where the time goes in v5:
time: 24 us; the launch traced here: 23.7 us
  starting transfers between devices  15.1 us (63%)
  waiting for transfers between devices  3.95 us (16%)
  Pallas kernels  3.86 us (16%)
  between operations  0.74 us (3%)
    all_to_all x1, starting transfers between devices, on_device(): partial = lax.all_to_all(partial, ('dp', 'ctx'), 0, 0)  5.29 us
    ppermute x3, starting transfers between devices, on_device(): kv.append(lax.ppermute(own_kv, both_axes, up_route(sections, size, d)))  4.66 us
    ppermute x4, starting transfers between devices, on_device(): lax.ppermute(kv_grad[d], both_axes, down_route(sections, size, d))  3.95 us
    ppermute x4, waiting for transfers between devices, on_device(): lax.ppermute(kv_grad[d], both_axes, down_route(sections, size, d))  3.93 us
    pallas_call x1, Pallas kernels, on_device(): pl.pallas_call(functools.partial(prepare_kernel, size), out_shape=(shape(...  2.86 us
    ppermute x1, starting transfers between devices, on_device(): lax.ppermute(packed, 'section', [(s, (s - 1) % sections) for s in range(s...  1.22 us
    pallas_call x1, Pallas kernels, on_device(): pl.pallas_call(output_kernel, out_shape=(shape(length, width, dtype=jnp.b...  0.86 us
  transfers between devices with their start and end apart: 9, of which 3 were waited for; matrix products, arithmetic and copies ran while one was open for 0% of the time, Pallas kernels for 1%

profile of v5, /device:TPU:0, one launch (start us, length us, event | category | flops | bytes accessed | tf_op | source)
XLA Modules:
  0.0 23.7 jit_solution(11550275350303008363)
XLA Ops:
  0.6 2.9 %prepare.1 = (bf16[256,128]{1,0:T(8,128)(2,1)S(1)}, f32[16,128]{1,0:T(8,128)S(1)}, bf16[128,2048]{1,0:T(8,128)(2,1)S(1)}, bf16[128,2048]{1,0:T(8,128)(2,1)S(1)},...) custom-call(f32[16,128]{1,0:T(8,128)} %bitcast.19, f32[16,128]{1,0:T(8,128)} %bitcast.20, f32[1,16]{1,0:T(1,128)} %refs_2_.1, ...), custom_call_target="tpu_custom_call" | custom-call | flops 33554432 | bytes 1572864 | tf_op jit(solution)/shard_map/prepare/pallas_call | solution.py:290
  3.5 0.5 %collective-permute-start.2 = (bf16[256,128]{1,0:T(8,128)(2,1)S(1)}, bf16[256,128]{1,0:T(8,128)(2,1)S(1)}, u32[]{:S(2)}, u32[]{:S(2)}) collective-permute-start(bf16[256,128]{1,0:T(8,128)(2,1)S(1)} %get-tuple-element.26.refs_3_), channel_id=1, source_target_pairs={{0,4},{1,5},{2,6},{3,0},{4,7},{5,1},{6,2},{7,3},{8,12},{9,13},{10,... | collective-permute-start | bytes 196616 | tf_op jit(solution)/shard_map/ppermute | solution.py:317
  4.0 4.1 %collective-permute-start.1 = (bf16[256,128]{1,0:T(8,128)(2,1)S(1)}, bf16[256,128]{1,0:T(8,128)(2,1)S(1)}, u32[]{:S(2)}, u32[]{:S(2)}) collective-permute-start(bf16[256,128]{1,0:T(8,128)(2,1)S(1)} %get-tuple-element.26.refs_3_), channel_id=1, source_target_pairs={{0,4},{1,5},{2,0},{3,1},{4,6},{5,7},{6,2},{7,3},{8,12},{9,13},{10,... | collective-permute-start | bytes 196616 | tf_op jit(solution)/shard_map/ppermute | solution.py:317
  8.2 0.0 collective-permute-start
  8.2 5.3 %all-to-all-start = ((f32[16,24,128]{2,1,0:T(8,128)}), f32[16,24,128]{2,1,0:T(8,128)S(1)}, u32[]{:S(2)}, u32[]{:S(2)}) async-start(f32[16,24,128]{2,1,0:T(8,128)} %get-tuple-element.33), calls=%async_computation | async-start | bytes 393216 | tf_op jit(solution)/shard_map/all_to_all | solution.py:318
  13.5 0.0 collective-permute-done.2.refs_6_
  13.5 0.0 collective-permute-done.1.refs_5_
  13.5 0.0 collective-permute-done.refs_4_
  13.5 0.1 score_grads.1
  13.5 1.3 %collective-permute-start.4 = (bf16[256,128]{1,0:T(8,128)(2,1)S(1)}, bf16[256,128]{1,0:T(8,128)(2,1)S(1)}, u32[]{:S(2)}, u32[]{:S(2)}) collective-permute-start(bf16[256,128]{1,0:T(8,128)(2,1)S(1)} %get-tuple-element.29), channel_id=1, source_target_pairs={{7,0},{15,8},{23,16},{31,24}} | collective-permute-start | bytes 196616 | tf_op jit(solution)/shard_map/ppermute | solution.py:332
  14.8 1.3 %collective-permute-start.5 = (bf16[256,128]{1,0:T(8,128)(2,1)S(1)}, bf16[256,128]{1,0:T(8,128)(2,1)S(1)}, u32[]{:S(2)}, u32[]{:S(2)}) collective-permute-start(bf16[256,128]{1,0:T(8,128)(2,1)S(1)} %get-tuple-element.30), channel_id=1, source_target_pairs={{6,0},{7,1},{14,8},{15,9},{22,16},{23,17},{30,24},{31,25}} | collective-permute-start | bytes 196616 | tf_op jit(solution)/shard_map/ppermute | solution.py:332
  16.1 1.3 %collective-permute-start.6 = (bf16[256,128]{1,0:T(8,128)(2,1)S(1)}, bf16[256,128]{1,0:T(8,128)(2,1)S(1)}, u32[]{:S(2)}, u32[]{:S(2)}) collective-permute-start(bf16[256,128]{1,0:T(8,128)(2,1)S(1)} %get-tuple-element.31), channel_id=1, source_target_pairs={{5,0},{6,1},{7,2},{13,8},{14,9},{15,10},{21,16},{22,17},{23,18},{2... | collective-permute-start | bytes 196616 | tf_op jit(solution)/shard_map/ppermute | solution.py:332
  17.4 0.1 collective-permute-start.7
  17.5 0.1 query_grads.1
  17.6 1.2 %collective-permute-start.3 = (bf16[128,2048]{1,0:T(8,128)(2,1)S(1)}, bf16[128,2048]{1,0:T(8,128)(2,1)S(1)}, u32[]{:S(2)}, u32[]{:S(2)}) collective-permute-start(bf16[128,2048]{1,0:T(8,128)(2,1)S(1)} %query_grads.1), channel_id=1, source_target_pairs={{0,4},{4,0},{1,5},{5,1},{2,6},{6,2},{3,7},{7,3},{8,12},{12,8},{9,1... | collective-permute-start | bytes 1572872 | tf_op jit(solution)/shard_map/ppermute | solution.py:345
  18.8 2.6 %collective-permute-done.4.refs_0_ = bf16[256,128]{1,0:T(8,128)(2,1)S(1)} collective-permute-done((bf16[256,128]{1,0:T(8,128)(2,1)S(1)}, bf16[256,128]{1,0:T(8,128)(2,1)S(1)}, u32[]{:S(2)}, u32[]{:S(2)}) %collective-permute-start.4) | collective-permute-done | bytes 65568 | tf_op jit(solution)/shard_map/ppermute | solution.py:332
  21.4 0.8 %collective-permute-done.5.refs_1_ = bf16[256,128]{1,0:T(8,128)(2,1)S(1)} collective-permute-done((bf16[256,128]{1,0:T(8,128)(2,1)S(1)}, bf16[256,128]{1,0:T(8,128)(2,1)S(1)}, u32[]{:S(2)}, u32[]{:S(2)}) %collective-permute-start.5) | collective-permute-done | bytes 65568 | tf_op jit(solution)/shard_map/ppermute | solution.py:332
  22.1 0.6 %collective-permute-done.6.refs_2_ = bf16[256,128]{1,0:T(8,128)(2,1)S(1)} collective-permute-done((bf16[256,128]{1,0:T(8,128)(2,1)S(1)}, bf16[256,128]{1,0:T(8,128)(2,1)S(1)}, u32[]{:S(2)}, u32[]{:S(2)}) %collective-permute-start.6) | collective-permute-done | bytes 65568 | tf_op jit(solution)/shard_map/ppermute | solution.py:332
  22.7 0.0 collective-permute-done.7.refs_3_
  22.7 0.0 all-to-all-done.refs_4_
  22.8 0.0 collective-permute-done.3.query
  22.8 0.9 %outputs.1 = (bf16[128,2048]{1,0:T(8,128)(2,1)}, bf16[128,128]{1,0:T(8,128)(2,1)}, bf16[128,128]{1,0:T(8,128)(2,1)}, f32[16,128]{1,0:T(8,128)}, f32[1,16]{1,0:T(1,128)}) custom-call(bf16[128,2048]{1,0:T(8,128)(2,1)S(1)} %collective-permute-done.3.query, bf16[256,128]{1,0:T(8,128)(2,1)S(1)} %get-tuple-element.34.kv_total, ...), custom_call_target="tpu_custom_call" | custom-call | tf_op jit(solution)/shard_map/outputs/pallas_call | solution.py:360
  (1 shorter events, 0.0 us)
Async XLA Ops:
  3.5 10.0 %collective-permute-start.2 = (bf16[256,128]{1,0:T(8,128)(2,1)S(1)}, bf16[256,128]{1,0:T(8,128)(2,1)S(1)}, u32[]{:S(2)}, u32[]{:S(2)}) collective-permute-start(bf16[256,128]{1,0:T(8,128)(2,1)S(1)} %get-tuple-element.26.refs_3_), channel_id=1, source_target_pairs={{0,4},{1,5},{2,6},{3,0},{4,7},{5,1},{6,2},{7,3},{8,12},{9,13},{10,... | collective-permute-start | bytes 196616 | tf_op jit(solution)/shard_map/ppermute | solution.py:317
  4.0 9.5 %collective-permute-start.1 = (bf16[256,128]{1,0:T(8,128)(2,1)S(1)}, bf16[256,128]{1,0:T(8,128)(2,1)S(1)}, u32[]{:S(2)}, u32[]{:S(2)}) collective-permute-start(bf16[256,128]{1,0:T(8,128)(2,1)S(1)} %get-tuple-element.26.refs_3_), channel_id=1, source_target_pairs={{0,4},{1,5},{2,0},{3,1},{4,6},{5,7},{6,2},{7,3},{8,12},{9,13},{10,... | collective-permute-start | bytes 196616 | tf_op jit(solution)/shard_map/ppermute | solution.py:317
  8.2 5.3 %collective-permute-start = (bf16[256,128]{1,0:T(8,128)(2,1)S(1)}, bf16[256,128]{1,0:T(8,128)(2,1)S(1)}, u32[]{:S(2)}, u32[]{:S(2)}) collective-permute-start(bf16[256,128]{1,0:T(8,128)(2,1)S(1)} %get-tuple-element.26.refs_3_), channel_id=1, source_target_pairs={{0,4},{1,0},{2,1},{3,2},{4,5},{5,6},{6,7},{7,3},{8,12},{9,8},{10,9... | collective-permute-start | bytes 196616 | tf_op jit(solution)/shard_map/ppermute | solution.py:317
  8.2 14.6 %all-to-all-start = ((f32[16,24,128]{2,1,0:T(8,128)}), f32[16,24,128]{2,1,0:T(8,128)S(1)}, u32[]{:S(2)}, u32[]{:S(2)}) async-start(f32[16,24,128]{2,1,0:T(8,128)} %get-tuple-element.33), calls=%async_computation | async-start | bytes 393216 | tf_op jit(solution)/shard_map/all_to_all | solution.py:318
  13.5 7.8 %collective-permute-start.4 = (bf16[256,128]{1,0:T(8,128)(2,1)S(1)}, bf16[256,128]{1,0:T(8,128)(2,1)S(1)}, u32[]{:S(2)}, u32[]{:S(2)}) collective-permute-start(bf16[256,128]{1,0:T(8,128)(2,1)S(1)} %get-tuple-element.29), channel_id=1, source_target_pairs={{7,0},{15,8},{23,16},{31,24}} | collective-permute-start | bytes 196616 | tf_op jit(solution)/shard_map/ppermute | solution.py:332
  14.8 7.3 %collective-permute-start.5 = (bf16[256,128]{1,0:T(8,128)(2,1)S(1)}, bf16[256,128]{1,0:T(8,128)(2,1)S(1)}, u32[]{:S(2)}, u32[]{:S(2)}) collective-permute-start(bf16[256,128]{1,0:T(8,128)(2,1)S(1)} %get-tuple-element.30), channel_id=1, source_target_pairs={{6,0},{7,1},{14,8},{15,9},{22,16},{23,17},{30,24},{31,25}} | collective-permute-start | bytes 196616 | tf_op jit(solution)/shard_map/ppermute | solution.py:332
  16.1 6.6 %collective-permute-start.6 = (bf16[256,128]{1,0:T(8,128)(2,1)S(1)}, bf16[256,128]{1,0:T(8,128)(2,1)S(1)}, u32[]{:S(2)}, u32[]{:S(2)}) collective-permute-start(bf16[256,128]{1,0:T(8,128)(2,1)S(1)} %get-tuple-element.31), channel_id=1, source_target_pairs={{5,0},{6,1},{7,2},{13,8},{14,9},{15,10},{21,16},{22,17},{23,18},{2... | collective-permute-start | bytes 196616 | tf_op jit(solution)/shard_map/ppermute | solution.py:332
  17.4 5.3 %collective-permute-start.7 = (bf16[256,128]{1,0:T(8,128)(2,1)S(1)}, bf16[256,128]{1,0:T(8,128)(2,1)S(1)}, u32[]{:S(2)}, u32[]{:S(2)}) collective-permute-start(bf16[256,128]{1,0:T(8,128)(2,1)S(1)} %get-tuple-element.32), channel_id=1, source_target_pairs={{4,0},{5,1},{6,2},{7,3},{0,4},{1,5},{2,6},{3,7},{12,8},{13,9},{14,... | collective-permute-start | bytes 196616 | tf_op jit(solution)/shard_map/ppermute | solution.py:332
  17.6 5.2 %collective-permute-start.3 = (bf16[128,2048]{1,0:T(8,128)(2,1)S(1)}, bf16[128,2048]{1,0:T(8,128)(2,1)S(1)}, u32[]{:S(2)}, u32[]{:S(2)}) collective-permute-start(bf16[128,2048]{1,0:T(8,128)(2,1)S(1)} %query_grads.1), channel_id=1, source_target_pairs={{0,4},{4,0},{1,5},{5,1},{2,6},{6,2},{3,7},{7,3},{8,12},{12,8},{9,1... | collective-permute-start | bytes 1572872 | tf_op jit(solution)/shard_map/ppermute | solution.py:345
